TPU v7x, 512 devices: a whole 4x8x8 slice. The times are simulated.
512 devices in a mesh: gx: 8 (over y_hi, core), gy: 8 (over z), gz: 8 (over y_lo, x).
Axes of the slice: x: 4, y: 8 (y_hi: 4, y_lo: 2; y = y_hi * 2 + y_lo), z: 8, core: 2. Of those that a mesh axis runs over, the one named last changes fastest.
Arguments:
- velocity: float32 [256, 256, 1024], P('gx', 'gy', 'gz'), may hold values from -6 to 6
- marker_logvisc: float32 [65536, 128], P(('gx', 'gy', 'gz')), may hold values from -3 to 3
- marker_force: float32 [65536, 128], P(('gx', 'gy', 'gz')), may hold values from -6 to 6
- marker_weight: float32 [65536, 128], P(('gx', 'gy', 'gz')), may hold values from 0.5 to 2
- marker_cell: int32 [65536, 128], P(('gx', 'gy', 'gz')), may hold values from 0 to 127
- block_count: int32 [65536], P(('gx', 'gy', 'gz')), may hold values from 1 to 128, 6291456 in all
- block_owner: int32 [65536, 1], P(('gx', 'gy', 'gz')), may hold values from 0 to 63; in each aligned block of 128 rows (0 to 127, 128 to 255, ...) at most 4 rows name the same one
- block_tile: int32 [65536], P(('gx', 'gy', 'gz')), may hold values from 0 to 1023
- eig_low: float32 [1], replicated, may hold values from 0.05 to 0.3
- eig_high: float32 [1], replicated, may hold values from 1.5 to 2.2
Outputs:
- smoothed: float32 [256, 256, 1024], P('gx', 'gy', 'gz')
- marker_velocity: float32 [65536, 128], P(('gx', 'gy', 'gz'))
Inputs may be any that keep to these rules, and one draw needn't show every extreme that they name: `block_owner`: among the 128 blocks of one device, no owner index is named by more than 4 blocks, a bound that some block reaches. `block_count`: slots at or after a block's count are padding; some block is full.
All inputs are finite; a program needn't handle non-finite values.
Results may differ from a plain program's by a relative error of at most 0.00017.
Values sent between devices are 32-bit elements; how exact they have to be, the bound alone decides.
A program may use at most 128 MiB of HBM per device.

v0:
```python
import math

import jax
import jax.numpy as jnp
from jax import lax
from jax.sharding import PartitionSpec as P

TILE_X = 4
TILE_Y = 4
TILE_Z = 8
SWEEPS = 3
TILE_CELLS = 128


def with_halo(cells, sides, width):
    for axis, dim in sides:
        count = lax.axis_size(axis)
        ends = count - 1
        head = lax.slice_in_dim(cells, 0, width, axis=dim)
        tail = lax.slice_in_dim(cells, cells.shape[dim] - width, cells.shape[dim], axis=dim)
        cells = jnp.concatenate(
            [
                lax.ppermute(tail, axis, [(i, (i + 1) % count) for i in range(ends)]),
                cells,
                lax.ppermute(head, axis, [((i + 1) % count, i) for i in range(ends)]),
            ],
            axis=dim,
        )
    return cells


def shifted(array, along, offset):
    index = [slice(1, extent - 1) for extent in array.shape]
    index[along] = slice(1 + offset, array.shape[along] - 1 + offset)
    return array[tuple(index)]


def operate(field, viscosity):
    centre_visc = shifted(viscosity, 0, 0)
    centre_field = shifted(field, 0, 0)
    flux_total = jnp.zeros_like(centre_field)
    diagonal = jnp.zeros_like(centre_field)
    for along in range(3):
        for offset in (1, -1):
            face = 0.5 * (centre_visc + shifted(viscosity, along, offset))
            diagonal = diagonal + face
            flux_total = flux_total + face * (centre_field - shifted(field, along, offset))
    return (flux_total, diagonal)


def smooth(velocity, rhs, viscosity, low, high):
    centre = (high + low) / 2
    half_width = (high - low) / 2
    sigma_ratio = centre / half_width
    rho_now = 1.0 / sigma_ratio
    visc_pad = with_halo(viscosity, (("gx", 0), ("gy", 1), ("gz", 2)), 1)
    field = velocity
    update = jnp.zeros_like(velocity)
    for sweep_index in range(SWEEPS):
        padded = with_halo(field, (("gx", 0), ("gy", 1), ("gz", 2)), 1)
        flux_total, diagonal = operate(padded, visc_pad)
        resid = rhs - flux_total
        if sweep_index == 0:
            update = resid / diagonal / centre
        else:
            rho_next = 1.0 / (2.0 * sigma_ratio - rho_now)
            update = rho_next * rho_now * update + 2.0 * rho_next / half_width * (resid / diagonal)
            rho_now = rho_next
        field = field + update
    return field


def one_hot_cells(cells):
    return (cells[..., None] == jnp.arange(TILE_CELLS, dtype=jnp.int32)).astype(jnp.float32)


def body(
    velocity,
    marker_logvisc,
    marker_force,
    marker_weight,
    marker_cell,
    block_count,
    block_owner,
    block_tile,
    eig_low,
    eig_high,
):
    blocks, slots = marker_weight.shape
    side_y = lax.axis_size("gy")
    side_z = lax.axis_size("gz")
    owners = side_y * side_z
    capacity = 2 * blocks // owners
    extent_x, extent_y, extent_z = velocity.shape
    tiles_x = extent_x // TILE_X
    tiles_y = extent_y // TILE_Y
    tiles_z = extent_z // TILE_Z
    tile_total = tiles_x * tiles_y * tiles_z
    group = math.gcd(blocks, 64)
    groups = blocks // group
    live = jnp.arange(slots, dtype=jnp.int32)[None, :] < block_count[:, None]
    weight = jnp.where(live, marker_weight, 0.0)
    channels = jnp.stack([weight, weight * marker_logvisc, weight * marker_force])
    channels = channels.reshape(3, groups, group, slots).transpose(1, 0, 2, 3)
    cells_grouped = marker_cell.reshape(groups, group, slots)

    def project(pair):
        cells, values = pair
        return jnp.einsum(
            "gsk,cgs->gck", one_hot_cells(cells), values, precision=lax.Precision.HIGHEST
        )

    block_sums = lax.map(project, (cells_grouped, channels)).reshape(blocks, 3, TILE_CELLS)
    owner = block_owner[:, 0]
    member = (owner[:, None] == jnp.arange(owners, dtype=jnp.int32)[None, :]).astype(jnp.int32)
    slot_of = jnp.sum(jnp.cumsum(member, axis=0) * member, axis=1) - 1
    outgoing = (
        jnp.zeros((owners, capacity, 3, TILE_CELLS), jnp.float32).at[owner, slot_of].set(block_sums)
    )
    tile_out = jnp.zeros((owners, capacity), jnp.int32).at[owner, slot_of].set(block_tile)
    tile_in = lax.all_to_all(
        tile_out, ("gy", "gz"), split_axis=0, concat_axis=0, tiled=True
    ).reshape(owners * capacity)
    incoming = lax.all_to_all(outgoing, ("gy", "gz"), split_axis=0, concat_axis=0, tiled=True)
    incoming = incoming.reshape(owners * capacity, 3 * TILE_CELLS)
    tile_acc = jax.ops.segment_sum(incoming, tile_in, tile_total)
    grid_sums = tile_acc.reshape(tiles_x, tiles_y, tiles_z, 3, TILE_X, TILE_Y, TILE_Z)
    grid_sums = grid_sums.transpose(3, 0, 4, 1, 5, 2, 6).reshape(3, extent_x, extent_y, extent_z)
    viscosity = jnp.exp(grid_sums[1] / (1.0 + grid_sums[0]))
    rhs = grid_sums[2]
    smoothed = smooth(velocity, rhs, viscosity, eig_low[0], eig_high[0])
    tile_view = smoothed.reshape(tiles_x, TILE_X, tiles_y, TILE_Y, tiles_z, TILE_Z)
    tile_view = tile_view.transpose(0, 2, 4, 1, 3, 5).reshape(tile_total, TILE_CELLS)
    returning = tile_view[tile_in].reshape(owners, capacity, TILE_CELLS)
    arrived = lax.all_to_all(returning, ("gy", "gz"), split_axis=0, concat_axis=0, tiled=True)
    block_values = arrived[owner, slot_of].reshape(groups, group, TILE_CELLS)

    def interpolate(pair):
        cells, values = pair
        return jnp.einsum(
            "gsk,gk->gs", one_hot_cells(cells), values, precision=lax.Precision.HIGHEST
        )

    picked = lax.map(interpolate, (cells_grouped, block_values)).reshape(blocks, slots)
    marker_velocity = jnp.where(live, picked, 0.0)
    return (smoothed, marker_velocity)


def solution(mesh):
    return jax.shard_map(
        body,
        mesh=mesh,
        in_specs=(
            P("gx", "gy", "gz"),
            P(("gx", "gy", "gz"), None),
            P(("gx", "gy", "gz"), None),
            P(("gx", "gy", "gz"), None),
            P(("gx", "gy", "gz"), None),
            P(("gx", "gy", "gz")),
            P(("gx", "gy", "gz"), None),
            P(("gx", "gy", "gz")),
            P(),
            P(),
        ),
        out_specs=(P("gx", "gy", "gz"), P(("gx", "gy", "gz"), None)),
        check_vma=False,
    )
```

profile of v0, /device:TPU:40, one launch (start us, length us, event | category | flops | bytes accessed | tf_op | source)
XLA Modules:
  0.0 302.7 jit_solution(18212709666926166616)
XLA Ops:
  3.1 11.0 %scatter_fusion = s32[64,4]{0,1:T(4,128)S(1)} fusion(s32[64,4]{0,1:T(4,128)S(1)} %broadcast_in_dim.25, s32[128]{0:T(128)S(1)} %get-tuple-element.70, s32[128]{0:T(128)} %param.21), kind=kCustom, calls=%fused_computation.2 | custom fusion | bytes 2560 | tf_op jit(solution)/shard_map/scatter | solution.py:120
  14.7 14.8 %all-to-all-start = ((s32[64,1,4]{2,1,0:T(1,128)}), s32[64,1,4]{2,1,0:T(1,128)S(1)}, u32[]{:S(2)}, u32[]{:S(2)}) async-start(s32[64,1,4]{2,1,0:T(1,128)} %copy.62), calls=%async_computation | async-start | bytes 65536 | tf_op jit(solution)/shard_map/all_to_all | solution.py:121
  31.6 7.5 %while.20 = (s32[]{:T(128)}, f32[2,64,3,128]{3,2,1,0:T(4,128)S(1)}, f32[2,3,64,128]{3,1,2,0:T(4,128)S(1)}, s32[2,64,128]{2,1,0:T(8,128)}, s32[]{:T(128)}) while((s32[]{:T(128)}, f32[2,64,3,128]{3,2,1,0:T(4,128)S(1)}, f32[2,3,64,128]{3,1,2,0:T(4,128)S(1)}, s32[2,64,128]{2,1,0:T(8,128)}, s32[]{:T(128)}) %tuple.58), condition=%wide.region_4.5_spmd, body=%wide.region_3.4_spmd.sunk | while | flops 38797312 | bytes 361537 | solution.py:113
  32.4 2.9 fusion.116
  36.1 2.9 fusion.116
  39.1 5.7 %scatter_fusion.1 = f32[64,4,3,128]{3,2,1,0:T(4,128)S(1)} fusion(f32[64,4,3,128]{3,2,1,0:T(4,128)S(1)} %broadcast_in_dim.44, s32[128]{0:T(128)S(1)} %get-tuple-element.70, f32[128,3,128]{2,1,0:T(4,128)S(1)} %bitcast.104), kind=kCustom, calls=%fused_computation.3 | custom fusion | bytes 590848 | tf_op jit(solution)/shard_map/scatter | solution.py:118
  45.7 11.2 %all-to-all-start.1 = ((f32[64,4,3,128]{3,1,2,0:T(4,128)}), f32[64,4,3,128]{3,1,2,0:T(4,128)S(1)}, u32[]{:S(2)}, u32[]{:S(2)}) async-start(f32[64,4,3,128]{3,1,2,0:T(4,128)} %copy.66), calls=%async_computation.1 | async-start | bytes 786432 | tf_op jit(solution)/shard_map/all_to_all | solution.py:124
  56.9 1.9 collective-permute-start.3
  58.9 5.8 %collective-permute-start.1 = (f32[1,32,128]{2,1,0:T(8,128)S(1)}, f32[1,32,128]{2,1,0:T(8,128)S(1)}, u32[]{:S(2)}, u32[]{:S(2)}) collective-permute-start(f32[1,32,128]{2,1,0:T(8,128)S(1)} %get-tuple-element.96), channel_id=1, source_target_pairs={{64,0},{128,64},{192,128},{256,192},{320,256},{384,320},{448,384},... | collective-permute-start | bytes 49160 | tf_op jit(solution)/shard_map/ppermute | solution.py:25
  68.3 4.5 %collective-permute-start.7 = (f32[34,1,128]{2,1,0:T(1,128)S(1)}, f32[34,1,128]{2,1,0:T(1,128)S(1)}, u32[]{:S(2)}, u32[]{:S(2)}) collective-permute-start(f32[34,1,128]{2,1,0:T(1,128)S(1)} %get-tuple-element.88), channel_id=1, source_target_pairs={{0,8},{8,16},{16,24},{24,32},{32,40},{40,48},{48,56},{1,9},{9,17},... | collective-permute-start | bytes 52232 | tf_op jit(solution)/shard_map/ppermute | solution.py:23
  73.1 2.5 scatter_custom_fusion.2
  76.1 7.1 %reshape.116 = f32[8,8,16,3,4,4,8]{2,1,0,6,5,4,3:T(8,128)} reshape(f32[1024,384]{0,1:T(8,128)S(1)} %copy.68) | data formatting | bytes 3145728 | tf_op jit(solution)/shard_map/reshape | solution.py:127
  83.1 10.0 %fusion.10 = (f32[1,8,4,8,4,16,8]{5,3,1,6,4,2,0:T(8,128)}, f32[1,8,4,8,4,16,8]{5,3,1,6,4,2,0:T(8,128)}) fusion(f32[3,8,4,8,4,16,8]{5,3,1,6,4,2,0:T(8,128)} %bitcast.93), kind=kLoop, calls=%fused_computation.22 | loop fusion | flops 262144 | bytes 2621440 | tf_op jit(solution)/shard_map/exp | solution.py:129
  93.1 7.1 %copy.70 = f32[1,8,4,8,4,16,8]{6,5,4,3,2,1,0:T(8,128)} copy(f32[1,8,4,8,4,16,8]{5,3,1,6,4,2,0:T(8,128)} %get-tuple-element.72) | data formatting | bytes 1048576 | tf_op jit(solution)/shard_map/exp | solution.py:129
  100.1 6.4 %exp.7 = f32[32,32,128]{2,1,0:T(8,128)S(1)} reshape(f32[1,8,4,8,4,16,8]{6,5,4,3,2,1,0:T(8,128)} %copy.70) | data formatting | bytes 1048576 | tf_op jit(solution)/shard_map/exp | solution.py:129
  106.6 1.9 collective-permute-start.2
  109.1 5.7 %collective-permute-start = (f32[1,32,128]{2,1,0:T(8,128)S(1)}, f32[1,32,128]{2,1,0:T(8,128)S(1)}, u32[]{:S(2)}, u32[]{:S(2)}) collective-permute-start(f32[1,32,128]{2,1,0:T(8,128)S(1)} %get-tuple-element.94), channel_id=1, source_target_pairs={{64,0},{128,64},{192,128},{256,192},{320,256},{384,320},{448,384},... | collective-permute-start | bytes 49160 | tf_op jit(solution)/shard_map/ppermute | solution.py:25
  117.7 4.7 %collective-permute-start.6 = (f32[34,1,128]{2,1,0:T(1,128)S(1)}, f32[34,1,128]{2,1,0:T(1,128)S(1)}, u32[]{:S(2)}, u32[]{:S(2)}) collective-permute-start(f32[34,1,128]{2,1,0:T(1,128)S(1)} %get-tuple-element.86), channel_id=1, source_target_pairs={{0,8},{8,16},{16,24},{24,32},{32,40},{40,48},{48,56},{1,9},{9,17},... | collective-permute-start | bytes 52232 | tf_op jit(solution)/shard_map/ppermute | solution.py:23
  123.0 4.6 %collective-permute-start.9 = (f32[34,34,1]{1,2,0:T(1,128)S(1)}, f32[34,34,1]{1,2,0:T(1,128)S(1)}, u32[]{:S(2)}, u32[]{:S(2)}) collective-permute-start(f32[34,34,1]{1,2,0:T(1,128)S(1)} %copy.73), channel_id=1, source_target_pairs={{1,0},{2,1},{3,2},{4,3},{5,4},{6,5},{7,6},{9,8},{10,9},{11,10},{12... | collective-permute-start | bytes 13880 | tf_op jit(solution)/shard_map/ppermute | solution.py:25
  130.5 6.0 %collective-permute-start.8 = (f32[34,34,1]{1,2,0:T(1,128)S(1)}, f32[34,34,1]{1,2,0:T(1,128)S(1)}, u32[]{:S(2)}, u32[]{:S(2)}) collective-permute-start(f32[34,34,1]{1,2,0:T(1,128)S(1)} %copy.71), channel_id=1, source_target_pairs={{1,0},{2,1},{3,2},{4,3},{5,4},{6,5},{7,6},{9,8},{10,9},{11,10},{12... | collective-permute-start | bytes 13880 | tf_op jit(solution)/shard_map/ppermute | solution.py:25
  142.5 7.1 %copy.69 = f32[1,8,4,8,4,16,8]{6,5,4,3,2,1,0:T(8,128)} copy(f32[1,8,4,8,4,16,8]{5,3,1,6,4,2,0:T(8,128)} %get-tuple-element.73) | data formatting | bytes 1048576 | tf_op jit(solution)/shard_map/slice | solution.py:130
  149.6 6.4 %squeeze.19 = f32[32,32,128]{2,1,0:T(8,128)S(1)} reshape(f32[1,8,4,8,4,16,8]{6,5,4,3,2,1,0:T(8,128)} %copy.69) | data formatting | bytes 1048576 | tf_op jit(solution)/shard_map/squeeze | solution.py:130
  156.7 5.9 %fusion.95 = (f32[32,32,128]{2,1,0:T(8,128)S(1)}, f32[32,32,128]{2,1,0:T(8,128)}) fusion(f32[32,32,128]{2,1,0:T(8,128)} %param.14, f32[]{:T(128)} %bitcast.25, f32[32,32,128]{2,1,0:T(8,128)S(1)} %squeeze.19, f32[34,1,128]{2,1,0:T(1,128)} %copy-done.12, f32[34,32,128]{2,1,0:T(8,128)} %copy-done.2, f32[34,1,128]{2,1,0:T(1,128)} %copy-done.13, ...), kind=kLoop, calls=%fused_computation.191 | loop fusion | flops 7602176 | bytes 3889220 | tf_op jit(solution)/shard_map/add | solution.py:69
  162.7 4.3 %collective-permute-start.12 = (f32[1,32,128]{2,1,0:T(8,128)S(1)}, f32[1,32,128]{2,1,0:T(8,128)S(1)}, u32[]{:S(2)}, u32[]{:S(2)}) collective-permute-start(f32[1,32,128]{2,1,0:T(8,128)S(1)} %get-tuple-element.93), channel_id=1, source_target_pairs={{64,0},{128,64},{192,128},{256,192},{320,256},{384,320},{448,384},... | collective-permute-start | bytes 49160 | tf_op jit(solution)/shard_map/ppermute | solution.py:25
  167.0 1.9 collective-permute-start.13
  169.0 5.2 %collective-permute-done.13 = f32[1,32,128]{2,1,0:T(8,128)S(1)} collective-permute-done((f32[1,32,128]{2,1,0:T(8,128)S(1)}, f32[1,32,128]{2,1,0:T(8,128)S(1)}, u32[]{:S(2)}, u32[]{:S(2)}) %collective-permute-start.13) | collective-permute-done | bytes 16416 | tf_op jit(solution)/shard_map/ppermute | solution.py:23
  175.5 4.5 %collective-permute-start.15 = (f32[34,1,128]{2,1,0:T(1,128)S(1)}, f32[34,1,128]{2,1,0:T(1,128)S(1)}, u32[]{:S(2)}, u32[]{:S(2)}) collective-permute-start(f32[34,1,128]{2,1,0:T(1,128)S(1)} %get-tuple-element.84), channel_id=1, source_target_pairs={{0,8},{8,16},{16,24},{24,32},{32,40},{40,48},{48,56},{1,9},{9,17},... | collective-permute-start | bytes 52232 | tf_op jit(solution)/shard_map/ppermute | solution.py:23
  184.4 5.7 %collective-permute-start.16 = (f32[34,34,1]{1,2,0:T(1,128)S(1)}, f32[34,34,1]{1,2,0:T(1,128)S(1)}, u32[]{:S(2)}, u32[]{:S(2)}) collective-permute-start(f32[34,34,1]{1,2,0:T(1,128)S(1)} %copy.79), channel_id=1, source_target_pairs={{1,0},{2,1},{3,2},{4,3},{5,4},{6,5},{7,6},{9,8},{10,9},{11,10},{12... | collective-permute-start | bytes 13880 | tf_op jit(solution)/shard_map/ppermute | solution.py:25
  194.9 4.4 %collective-permute-done.17 = f32[34,34,1]{1,2,0:T(1,128)S(1)} collective-permute-done((f32[34,34,1]{1,2,0:T(1,128)S(1)}, f32[34,34,1]{1,2,0:T(1,128)S(1)}, u32[]{:S(2)}, u32[]{:S(2)}) %collective-permute-start.17) | collective-permute-done | bytes 4656 | tf_op jit(solution)/shard_map/ppermute | solution.py:23
  200.5 5.0 %fusion.93 = (f32[32,32,128]{2,1,0:T(8,128)S(1)}, f32[32,32,128]{2,1,0:T(8,128)}) fusion(f32[32,32,128]{2,1,0:T(8,128)S(1)} %get-tuple-element.66, f32[32,32,128]{2,1,0:T(8,128)} %copy-done, f32[34,1,128]{2,1,0:T(1,128)} %copy-done.14, f32[1,32,128]{2,1,0:T(8,128)} %copy-done.10, f32[1,32,128]{2,1,0:T(8,128)} %copy-done.11, f32[34,1,128]{2,1,0:T(1,128)} %copy-done.15, ...), kind=kLoop, calls=%fused_computation.190 | loop fusion | flops 8912896 | bytes 3856456 | tf_op jit(solution)/shard_map/add | solution.py:69
  208.1 2.4 collective-permute-start.19
  211.5 4.1 %collective-permute-done.19 = f32[1,32,128]{2,1,0:T(8,128)} collective-permute-done((f32[1,32,128]{2,1,0:T(8,128)}, f32[1,32,128]{2,1,0:T(8,128)}, u32[]{:S(2)}, u32[]{:S(2)}) %collective-permute-start.19) | collective-permute-done | bytes 16416 | tf_op jit(solution)/shard_map/ppermute | solution.py:23
  217.6 4.8 %collective-permute-start.21 = (f32[34,1,128]{2,1,0:T(1,128)S(1)}, f32[34,1,128]{2,1,0:T(1,128)S(1)}, u32[]{:S(2)}, u32[]{:S(2)}) collective-permute-start(f32[34,1,128]{2,1,0:T(1,128)S(1)} %get-tuple-element.82), channel_id=1, source_target_pairs={{0,8},{8,16},{16,24},{24,32},{32,40},{40,48},{48,56},{1,9},{9,17},... | collective-permute-start | bytes 52232 | tf_op jit(solution)/shard_map/ppermute | solution.py:23
  226.6 2.0 copy.83
  230.5 2.0 copy.85
  232.6 4.1 %collective-permute-start.23 = (f32[34,34,1]{1,2,0:T(1,128)}, f32[34,34,1]{1,2,0:T(1,128)}, u32[]{:S(2)}, u32[]{:S(2)}) collective-permute-start(f32[34,34,1]{1,2,0:T(1,128)} %copy.85), channel_id=1, source_target_pairs={{0,1},{1,2},{2,3},{3,4},{4,5},{5,6},{6,7},{8,9},{9,10},{10,11},{11... | collective-permute-start | bytes 13880 | tf_op jit(solution)/shard_map/ppermute | solution.py:23
  236.7 1.9 copy.84
  238.7 2.0 collective-permute-done.23
  240.6 1.9 copy.86
  242.6 5.0 %fusion.20 = f32[32,32,128]{2,1,0:T(8,128)} fusion(f32[32,32,128]{2,1,0:T(8,128)S(1)} %get-tuple-element.64, f32[32,32,128]{2,1,0:T(8,128)S(1)} %copy-done.1, f32[34,34,1]{2,1,0:T(8,128)} %copy.86, f32[34,1,128]{2,1,0:T(1,128)} %copy-done.16, f32[34,1,128]{2,1,0:T(1,128)} %copy-done.17, f32[1,32,128]{2,1,0:T(8,128)} %collective-permute-done.18, ...), kind=kLoop, calls=%fused_computation.37 | loop fusion | flops 8912896 | bytes 3332168 | tf_op jit(solution)/shard_map/add | solution.py:69
  247.6 7.0 %reshape.117 = f32[8,4,8,4,16,8]{5,4,3,2,1,0:T(8,128)} reshape(f32[32,32,128]{2,1,0:T(8,128)} %fusion.20) | data formatting | bytes 1048576 | tf_op jit(solution)/shard_map/reshape | solution.py:132
  254.6 6.9 %copy.87 = f32[8,8,16,4,4,8]{2,1,0,5,4,3:T(8,128)} copy(f32[8,8,16,4,4,8]{5,2,4,1,3,0:T(8,128)} %bitcast.94) | data formatting | bytes 1048576 | tf_op jit(solution)/shard_map/transpose | solution.py:133
  261.6 4.7 %reshape.118 = f32[1024,128]{0,1:T(8,128)S(1)} reshape(f32[8,8,16,4,4,8]{2,1,0,5,4,3:T(8,128)} %copy.87) | data formatting | bytes 1048576 | tf_op jit(solution)/shard_map/reshape | solution.py:133
  267.8 14.4 %all-to-all-start.2 = ((f32[64,4,128]{2,1,0:T(4,128)}), f32[64,4,128]{2,1,0:T(4,128)S(1)}, u32[]{:S(2)}, u32[]{:S(2)}) async-start(f32[64,4,128]{2,1,0:T(4,128)} %bitcast.29), calls=%async_computation.2 | async-start | bytes 262144 | tf_op jit(solution)/shard_map/all_to_all | solution.py:135
  282.3 10.6 %all-to-all-done.2 = f32[64,4,128]{2,1,0:T(4,128)S(1)} async-done(((f32[64,4,128]{2,1,0:T(4,128)}), f32[64,4,128]{2,1,0:T(4,128)S(1)}, u32[]{:S(2)}, u32[]{:S(2)}) %all-to-all-start.2) | async-done | bytes 131104 | tf_op jit(solution)/shard_map/all_to_all | solution.py:135
  293.9 8.1 %while.21 = (s32[]{:T(128)}, f32[2,64,128]{2,1,0:T(8,128)S(1)}, s32[2,64,128]{2,1,0:T(8,128)S(1)}, f32[2,64,128]{2,1,0:T(8,128)S(1)}, s32[]{:T(128)}) while((s32[]{:T(128)}, f32[2,64,128]{2,1,0:T(8,128)S(1)}, s32[2,64,128]{2,1,0:T(8,128)S(1)}, f32[2,64,128]{2,1,0:T(8,128)S(1)}, s32[]{:T(128)}) %tuple.60), condition=%wide.region_8.9_spmd, body=%wide.region_7.8_spmd.sunk | while | flops 13631490 | bytes 294985 | solution.py:144
  293.9 4.0 %fusion.118 = f32[64,1,128]{2,1,0:T(1,128)S(1)} fusion(f32[64,128,1]{1,2,0:T(1,128)S(1)} %bitcast.99, s32[64,128]{1,0:T(8,128)S(1)} %dynamic-slice_bitcast_fusion.5), kind=kOutput, calls=%fused_computation.15.clone.1 | convolution fusion | flops 13631488 | bytes 98304 | tf_op jit(solution)/shard_map/while/body/eval_jaxpr/gsk,gk->gs/dot_general | solution.py:140
  298.0 4.0 %fusion.118 = f32[64,1,128]{2,1,0:T(1,128)S(1)} fusion(f32[64,128,1]{1,2,0:T(1,128)S(1)} %bitcast.99, s32[64,128]{1,0:T(8,128)S(1)} %dynamic-slice_bitcast_fusion.5), kind=kOutput, calls=%fused_computation.15.clone.1 | convolution fusion | flops 13631488 | bytes 98304 | tf_op jit(solution)/shard_map/while/body/eval_jaxpr/gsk,gk->gs/dot_general | solution.py:140
  (140 shorter events, 50.2 us)
Async XLA Ops:
  14.7 31.0 %all-to-all-start = ((s32[64,1,4]{2,1,0:T(1,128)}), s32[64,1,4]{2,1,0:T(1,128)S(1)}, u32[]{:S(2)}, u32[]{:S(2)}) async-start(s32[64,1,4]{2,1,0:T(1,128)} %copy.62), calls=%async_computation | async-start | bytes 65536 | tf_op jit(solution)/shard_map/all_to_all | solution.py:121
  31.5 25.4 %copy-start.4 = (f32[32,32,128]{2,1,0:T(8,128)S(1)}, f32[32,32,128]{2,1,0:T(8,128)}, u32[]{:S(2)}) copy-start(f32[32,32,128]{2,1,0:T(8,128)} %param.14) | copy-start | bytes 1572868
  45.7 27.4 %copy-start.6 = (s32[64,1,4]{2,1,0:T(1,128)}, s32[64,1,4]{2,1,0:T(1,128)S(1)}, u32[]{:S(2)}) copy-start(s32[64,1,4]{2,1,0:T(1,128)S(1)} %all-to-all-done) | copy-start | bytes 3076
  45.7 27.2 %all-to-all-start.1 = ((f32[64,4,3,128]{3,1,2,0:T(4,128)}), f32[64,4,3,128]{3,1,2,0:T(4,128)S(1)}, u32[]{:S(2)}, u32[]{:S(2)}) async-start(f32[64,4,3,128]{3,1,2,0:T(4,128)} %copy.66), calls=%async_computation.1 | async-start | bytes 786432 | tf_op jit(solution)/shard_map/all_to_all | solution.py:124
  56.9 9.1 %collective-permute-start.3 = (f32[1,32,128]{2,1,0:T(8,128)S(1)}, f32[1,32,128]{2,1,0:T(8,128)S(1)}, u32[]{:S(2)}, u32[]{:S(2)}) collective-permute-start(f32[1,32,128]{2,1,0:T(8,128)S(1)} %get-tuple-element.97), channel_id=1, source_target_pairs={{0,64},{64,128},{128,192},{192,256},{256,320},{320,384},{384,448},... | collective-permute-start | bytes 49160 | tf_op jit(solution)/shard_map/ppermute | solution.py:23
  58.9 7.3 %collective-permute-start.1 = (f32[1,32,128]{2,1,0:T(8,128)S(1)}, f32[1,32,128]{2,1,0:T(8,128)S(1)}, u32[]{:S(2)}, u32[]{:S(2)}) collective-permute-start(f32[1,32,128]{2,1,0:T(8,128)S(1)} %get-tuple-element.96), channel_id=1, source_target_pairs={{64,0},{128,64},{192,128},{256,192},{320,256},{384,320},{448,384},... | collective-permute-start | bytes 49160 | tf_op jit(solution)/shard_map/ppermute | solution.py:25
  66.1 7.0 %copy-start.18 = (f32[1,32,128]{2,1,0:T(8,128)}, f32[1,32,128]{2,1,0:T(8,128)S(1)}, u32[]{:S(2)}) copy-start(f32[1,32,128]{2,1,0:T(8,128)S(1)} %collective-permute-done.3) | copy-start | bytes 49156
  66.2 6.9 %copy-start.19 = (f32[1,32,128]{2,1,0:T(8,128)}, f32[1,32,128]{2,1,0:T(8,128)S(1)}, u32[]{:S(2)}) copy-start(f32[1,32,128]{2,1,0:T(8,128)S(1)} %collective-permute-done.1) | copy-start | bytes 49156
  66.2 0.8 copy-start.2
  67.0 41.5 %collective-permute-start.5 = (f32[34,1,128]{2,1,0:T(1,128)S(1)}, f32[34,1,128]{2,1,0:T(1,128)S(1)}, u32[]{:S(2)}, u32[]{:S(2)}) collective-permute-start(f32[34,1,128]{2,1,0:T(1,128)S(1)} %get-tuple-element.89), channel_id=1, source_target_pairs={{8,0},{16,8},{24,16},{32,24},{40,32},{48,40},{56,48},{9,1},{17,9},... | collective-permute-start | bytes 52232 | tf_op jit(solution)/shard_map/ppermute | solution.py:25
  68.3 40.2 %collective-permute-start.7 = (f32[34,1,128]{2,1,0:T(1,128)S(1)}, f32[34,1,128]{2,1,0:T(1,128)S(1)}, u32[]{:S(2)}, u32[]{:S(2)}) collective-permute-start(f32[34,1,128]{2,1,0:T(1,128)S(1)} %get-tuple-element.88), channel_id=1, source_target_pairs={{0,8},{8,16},{16,24},{24,32},{32,40},{40,48},{48,56},{1,9},{9,17},... | collective-permute-start | bytes 52232 | tf_op jit(solution)/shard_map/ppermute | solution.py:23
  100.1 8.4 %copy-start.3 = (f32[34,32,128]{2,1,0:T(8,128)S(1)}, f32[34,32,128]{2,1,0:T(8,128)}, u32[]{:S(2)}) copy-start(f32[34,32,128]{2,1,0:T(8,128)} %copy-done.2) | copy-start | bytes 1671172
  106.6 8.3 %collective-permute-start.2 = (f32[1,32,128]{2,1,0:T(8,128)S(1)}, f32[1,32,128]{2,1,0:T(8,128)S(1)}, u32[]{:S(2)}, u32[]{:S(2)}) collective-permute-start(f32[1,32,128]{2,1,0:T(8,128)S(1)} %get-tuple-element.95), channel_id=1, source_target_pairs={{0,64},{64,128},{128,192},{192,256},{256,320},{320,384},{384,448},... | collective-permute-start | bytes 49160 | tf_op jit(solution)/shard_map/ppermute | solution.py:23
  108.5 0.6 copy-start.12
  108.6 21.6 %copy-start.13 = (f32[34,1,128]{2,1,0:T(1,128)}, f32[34,1,128]{2,1,0:T(1,128)S(1)}, u32[]{:S(2)}) copy-start(f32[34,1,128]{2,1,0:T(1,128)S(1)} %collective-permute-done.7) | copy-start | bytes 52228
  109.1 7.2 %collective-permute-start = (f32[1,32,128]{2,1,0:T(8,128)S(1)}, f32[1,32,128]{2,1,0:T(8,128)S(1)}, u32[]{:S(2)}, u32[]{:S(2)}) collective-permute-start(f32[1,32,128]{2,1,0:T(8,128)S(1)} %get-tuple-element.94), channel_id=1, source_target_pairs={{64,0},{128,64},{192,128},{256,192},{320,256},{384,320},{448,384},... | collective-permute-start | bytes 49160 | tf_op jit(solution)/shard_map/ppermute | solution.py:25
  114.9 2.7 copy-start.8
  116.3 1.3 copy-start.9
  116.3 13.5 %collective-permute-start.4 = (f32[34,1,128]{2,1,0:T(1,128)S(1)}, f32[34,1,128]{2,1,0:T(1,128)S(1)}, u32[]{:S(2)}, u32[]{:S(2)}) collective-permute-start(f32[34,1,128]{2,1,0:T(1,128)S(1)} %get-tuple-element.87), channel_id=1, source_target_pairs={{8,0},{16,8},{24,16},{32,24},{40,32},{48,40},{56,48},{9,1},{17,9},... | collective-permute-start | bytes 52232 | tf_op jit(solution)/shard_map/ppermute | solution.py:25
  117.7 12.2 %collective-permute-start.6 = (f32[34,1,128]{2,1,0:T(1,128)S(1)}, f32[34,1,128]{2,1,0:T(1,128)S(1)}, u32[]{:S(2)}, u32[]{:S(2)}) collective-permute-start(f32[34,1,128]{2,1,0:T(1,128)S(1)} %get-tuple-element.86), channel_id=1, source_target_pairs={{0,8},{8,16},{16,24},{24,32},{32,40},{40,48},{48,56},{1,9},{9,17},... | collective-permute-start | bytes 52232 | tf_op jit(solution)/shard_map/ppermute | solution.py:23
  123.0 17.1 %collective-permute-start.9 = (f32[34,34,1]{1,2,0:T(1,128)S(1)}, f32[34,34,1]{1,2,0:T(1,128)S(1)}, u32[]{:S(2)}, u32[]{:S(2)}) collective-permute-start(f32[34,34,1]{1,2,0:T(1,128)S(1)} %copy.73), channel_id=1, source_target_pairs={{1,0},{2,1},{3,2},{4,3},{5,4},{6,5},{7,6},{9,8},{10,9},{11,10},{12... | collective-permute-start | bytes 13880 | tf_op jit(solution)/shard_map/ppermute | solution.py:25
  127.9 13.4 %collective-permute-start.11 = (f32[34,34,1]{1,2,0:T(1,128)S(1)}, f32[34,34,1]{1,2,0:T(1,128)S(1)}, u32[]{:S(2)}, u32[]{:S(2)}) collective-permute-start(f32[34,34,1]{1,2,0:T(1,128)S(1)} %copy.77), channel_id=1, source_target_pairs={{0,1},{1,2},{2,3},{3,4},{4,5},{5,6},{6,7},{8,9},{9,10},{10,11},{11... | collective-permute-start | bytes 13880 | tf_op jit(solution)/shard_map/ppermute | solution.py:23
  129.8 19.8 %copy-start.7 = (f32[34,1,128]{2,1,0:T(1,128)}, f32[34,1,128]{2,1,0:T(1,128)S(1)}, u32[]{:S(2)}) copy-start(f32[34,1,128]{2,1,0:T(1,128)S(1)} %collective-permute-done.6) | copy-start | bytes 52228
  130.5 25.5 %collective-permute-start.8 = (f32[34,34,1]{1,2,0:T(1,128)S(1)}, f32[34,34,1]{1,2,0:T(1,128)S(1)}, u32[]{:S(2)}, u32[]{:S(2)}) collective-permute-start(f32[34,34,1]{1,2,0:T(1,128)S(1)} %copy.71), channel_id=1, source_target_pairs={{1,0},{2,1},{3,2},{4,3},{5,4},{6,5},{7,6},{9,8},{10,9},{11,10},{12... | collective-permute-start | bytes 13880 | tf_op jit(solution)/shard_map/ppermute | solution.py:25
  136.9 19.5 %collective-permute-start.10 = (f32[34,34,1]{1,2,0:T(1,128)S(1)}, f32[34,34,1]{1,2,0:T(1,128)S(1)}, u32[]{:S(2)}, u32[]{:S(2)}) collective-permute-start(f32[34,34,1]{1,2,0:T(1,128)S(1)} %copy.75), channel_id=1, source_target_pairs={{0,1},{1,2},{2,3},{3,4},{4,5},{5,6},{6,7},{8,9},{9,10},{10,11},{11... | collective-permute-start | bytes 13880 | tf_op jit(solution)/shard_map/ppermute | solution.py:23
  156.0 18.2 %copy-start = (f32[32,32,128]{2,1,0:T(8,128)}, f32[32,32,128]{2,1,0:T(8,128)S(1)}, u32[]{:S(2)}) copy-start(f32[32,32,128]{2,1,0:T(8,128)S(1)} %squeeze.19) | copy-start | bytes 1572868
  162.7 6.3 %collective-permute-start.12 = (f32[1,32,128]{2,1,0:T(8,128)S(1)}, f32[1,32,128]{2,1,0:T(8,128)S(1)}, u32[]{:S(2)}, u32[]{:S(2)}) collective-permute-start(f32[1,32,128]{2,1,0:T(8,128)S(1)} %get-tuple-element.93), channel_id=1, source_target_pairs={{64,0},{128,64},{192,128},{256,192},{320,256},{384,320},{448,384},... | collective-permute-start | bytes 49160 | tf_op jit(solution)/shard_map/ppermute | solution.py:25
  167.0 7.2 %collective-permute-start.13 = (f32[1,32,128]{2,1,0:T(8,128)S(1)}, f32[1,32,128]{2,1,0:T(8,128)S(1)}, u32[]{:S(2)}, u32[]{:S(2)}) collective-permute-start(f32[1,32,128]{2,1,0:T(8,128)S(1)} %get-tuple-element.92), channel_id=1, source_target_pairs={{0,64},{64,128},{128,192},{192,256},{256,320},{320,384},{384,448},... | collective-permute-start | bytes 49160 | tf_op jit(solution)/shard_map/ppermute | solution.py:23
  168.9 12.6 %copy-start.10 = (f32[1,32,128]{2,1,0:T(8,128)}, f32[1,32,128]{2,1,0:T(8,128)S(1)}, u32[]{:S(2)}) copy-start(f32[1,32,128]{2,1,0:T(8,128)S(1)} %collective-permute-done.12) | copy-start | bytes 49156
  174.2 7.3 %copy-start.11 = (f32[1,32,128]{2,1,0:T(8,128)}, f32[1,32,128]{2,1,0:T(8,128)S(1)}, u32[]{:S(2)}) copy-start(f32[1,32,128]{2,1,0:T(8,128)S(1)} %collective-permute-done.13) | copy-start | bytes 49156
  174.2 5.9 %collective-permute-start.14 = (f32[34,1,128]{2,1,0:T(1,128)S(1)}, f32[34,1,128]{2,1,0:T(1,128)S(1)}, u32[]{:S(2)}, u32[]{:S(2)}) collective-permute-start(f32[34,1,128]{2,1,0:T(1,128)S(1)} %get-tuple-element.85), channel_id=1, source_target_pairs={{8,0},{16,8},{24,16},{32,24},{40,32},{48,40},{56,48},{9,1},{17,9},... | collective-permute-start | bytes 52232 | tf_op jit(solution)/shard_map/ppermute | solution.py:25
  175.5 6.0 %collective-permute-start.15 = (f32[34,1,128]{2,1,0:T(1,128)S(1)}, f32[34,1,128]{2,1,0:T(1,128)S(1)}, u32[]{:S(2)}, u32[]{:S(2)}) collective-permute-start(f32[34,1,128]{2,1,0:T(1,128)S(1)} %get-tuple-element.84), channel_id=1, source_target_pairs={{0,8},{8,16},{16,24},{24,32},{32,40},{40,48},{48,56},{1,9},{9,17},... | collective-permute-start | bytes 52232 | tf_op jit(solution)/shard_map/ppermute | solution.py:23
  180.1 20.4 %copy-start.14 = (f32[34,1,128]{2,1,0:T(1,128)}, f32[34,1,128]{2,1,0:T(1,128)S(1)}, u32[]{:S(2)}) copy-start(f32[34,1,128]{2,1,0:T(1,128)S(1)} %collective-permute-done.14) | copy-start | bytes 52228
  181.5 19.0 %copy-start.15 = (f32[34,1,128]{2,1,0:T(1,128)}, f32[34,1,128]{2,1,0:T(1,128)S(1)}, u32[]{:S(2)}) copy-start(f32[34,1,128]{2,1,0:T(1,128)S(1)} %collective-permute-done.15) | copy-start | bytes 52228
  184.4 9.3 %collective-permute-start.16 = (f32[34,34,1]{1,2,0:T(1,128)S(1)}, f32[34,34,1]{1,2,0:T(1,128)S(1)}, u32[]{:S(2)}, u32[]{:S(2)}) collective-permute-start(f32[34,34,1]{1,2,0:T(1,128)S(1)} %copy.79), channel_id=1, source_target_pairs={{1,0},{2,1},{3,2},{4,3},{5,4},{6,5},{7,6},{9,8},{10,9},{11,10},{12... | collective-permute-start | bytes 13880 | tf_op jit(solution)/shard_map/ppermute | solution.py:25
  191.5 7.7 %collective-permute-start.17 = (f32[34,34,1]{1,2,0:T(1,128)S(1)}, f32[34,34,1]{1,2,0:T(1,128)S(1)}, u32[]{:S(2)}, u32[]{:S(2)}) collective-permute-start(f32[34,34,1]{1,2,0:T(1,128)S(1)} %copy.81), channel_id=1, source_target_pairs={{0,1},{1,2},{2,3},{3,4},{4,5},{5,6},{6,7},{8,9},{9,10},{10,11},{11... | collective-permute-start | bytes 13880 | tf_op jit(solution)/shard_map/ppermute | solution.py:23
  205.6 37.0 %copy-start.1 = (f32[32,32,128]{2,1,0:T(8,128)S(1)}, f32[32,32,128]{2,1,0:T(8,128)}, u32[]{:S(2)}) copy-start(f32[32,32,128]{2,1,0:T(8,128)} %copy-done) | copy-start | bytes 1572868
  206.2 5.3 %collective-permute-start.18 = (f32[1,32,128]{2,1,0:T(8,128)}, f32[1,32,128]{2,1,0:T(8,128)}, u32[]{:S(2)}, u32[]{:S(2)}) collective-permute-start(f32[1,32,128]{2,1,0:T(8,128)} %get-tuple-element.91), channel_id=1, source_target_pairs={{64,0},{128,64},{192,128},{256,192},{320,256},{384,320},{448,384},... | collective-permute-start | bytes 49160 | tf_op jit(solution)/shard_map/ppermute | solution.py:25
  208.1 7.5 %collective-permute-start.19 = (f32[1,32,128]{2,1,0:T(8,128)}, f32[1,32,128]{2,1,0:T(8,128)}, u32[]{:S(2)}, u32[]{:S(2)}) collective-permute-start(f32[1,32,128]{2,1,0:T(8,128)} %get-tuple-element.90), channel_id=1, source_target_pairs={{0,64},{64,128},{128,192},{192,256},{256,320},{320,384},{384,448},... | collective-permute-start | bytes 49160 | tf_op jit(solution)/shard_map/ppermute | solution.py:23
  216.3 6.2 %collective-permute-start.20 = (f32[34,1,128]{2,1,0:T(1,128)S(1)}, f32[34,1,128]{2,1,0:T(1,128)S(1)}, u32[]{:S(2)}, u32[]{:S(2)}) collective-permute-start(f32[34,1,128]{2,1,0:T(1,128)S(1)} %get-tuple-element.83), channel_id=1, source_target_pairs={{8,0},{16,8},{24,16},{32,24},{40,32},{48,40},{56,48},{9,1},{17,9},... | collective-permute-start | bytes 52232 | tf_op jit(solution)/shard_map/ppermute | solution.py:25
  217.6 6.3 %collective-permute-start.21 = (f32[34,1,128]{2,1,0:T(1,128)S(1)}, f32[34,1,128]{2,1,0:T(1,128)S(1)}, u32[]{:S(2)}, u32[]{:S(2)}) collective-permute-start(f32[34,1,128]{2,1,0:T(1,128)S(1)} %get-tuple-element.82), channel_id=1, source_target_pairs={{0,8},{8,16},{16,24},{24,32},{32,40},{40,48},{48,56},{1,9},{9,17},... | collective-permute-start | bytes 52232 | tf_op jit(solution)/shard_map/ppermute | solution.py:23
  222.5 1.4 copy-start.16
  223.9 0.6 copy-start.17
  228.6 8.1 %collective-permute-start.22 = (f32[34,34,1]{1,2,0:T(1,128)}, f32[34,34,1]{1,2,0:T(1,128)}, u32[]{:S(2)}, u32[]{:S(2)}) collective-permute-start(f32[34,34,1]{1,2,0:T(1,128)} %copy.83), channel_id=1, source_target_pairs={{1,0},{2,1},{3,2},{4,3},{5,4},{6,5},{7,6},{9,8},{10,9},{11,10},{12... | collective-permute-start | bytes 13880 | tf_op jit(solution)/shard_map/ppermute | solution.py:25
  232.6 8.1 %collective-permute-start.23 = (f32[34,34,1]{1,2,0:T(1,128)}, f32[34,34,1]{1,2,0:T(1,128)}, u32[]{:S(2)}, u32[]{:S(2)}) collective-permute-start(f32[34,34,1]{1,2,0:T(1,128)} %copy.85), channel_id=1, source_target_pairs={{0,1},{1,2},{2,3},{3,4},{4,5},{5,6},{6,7},{8,9},{9,10},{10,11},{11... | collective-permute-start | bytes 13880 | tf_op jit(solution)/shard_map/ppermute | solution.py:23
  261.6 32.3 %copy-start.5 = (s32[2,64,128]{2,1,0:T(8,128)S(1)}, s32[2,64,128]{2,1,0:T(8,128)}, u32[]{:S(2)}) copy-start(s32[2,64,128]{2,1,0:T(8,128)} %get-tuple-element.179) | copy-start | bytes 196612
  267.8 25.0 %all-to-all-start.2 = ((f32[64,4,128]{2,1,0:T(4,128)}), f32[64,4,128]{2,1,0:T(4,128)S(1)}, u32[]{:S(2)}, u32[]{:S(2)}) async-start(f32[64,4,128]{2,1,0:T(4,128)} %bitcast.29), calls=%async_computation.2 | async-start | bytes 262144 | tf_op jit(solution)/shard_map/all_to_all | solution.py:135
  293.9 8.1 %copy-start.20 = (s32[128]{0:T(128)S(1)}, s32[128]{0:T(128)}, u32[]{:S(2)}) copy-start(s32[128]{0:T(128)} %param.19) | copy-start | bytes 1540
where the time goes:
time: 305 us; the launch traced here: 303 us
  starting transfers between devices  118 us (39%)
  local copies, waits for them, and re-layouts  101 us (33%)
  other arithmetic  36.2 us (12%)
  waiting for transfers between devices  30.5 us (10%)
  matrix products  13.9 us (5%)
    ppermute x12, starting transfers between devices, with_halo(): lax.ppermute(head, axis, [((i + 1) % count, i) for i in range(ends)])  41.2 us
    ppermute x12, starting transfers between devices, with_halo(): lax.ppermute(tail, axis, [(i, (i + 1) % count) for i in range(ends)])  36.7 us
    ppermute x12, waiting for transfers between devices, with_halo(): lax.ppermute(tail, axis, [(i, (i + 1) % count) for i in range(ends)])  18.5 us
    add x3, other arithmetic, smooth(): field = field + update  16 us
    all_to_all x1, starting transfers between devices, body(): lax.all_to_all(tile_out, ('gy', 'gz'), split_axis=0, concat_axis=0, tiled...  14.8 us
    all_to_all x1, starting transfers between devices, body(): lax.all_to_all(returning, ('gy', 'gz'), split_axis=0, concat_axis=0, tile...  14.4 us
    exp x2, local copies, waits for them, and re-layouts, body(): viscosity = jnp.exp(grid_sums[1] / (1.0 + grid_sums[0]))  13.5 us
    all_to_all x1, starting transfers between devices, body(): lax.all_to_all(outgoing, ('gy', 'gz'), split_axis=0, concat_axis=0, tiled...  11.2 us
  transfers between devices with their start and end apart: 27, of which 8 were waited for; matrix products, arithmetic and copies ran while one was open for 25% of the time, Pallas kernels for 0%

commit v1 on v0

v1 whole, which is shorter than its diff:
```python
import functools
import math

import jax
import jax.numpy as jnp
from jax import lax
from jax.experimental import pallas as pl
from jax.experimental.pallas import tpu as pltpu
from jax.sharding import PartitionSpec as P

TILE_CELLS = 128
SWEEPS = 3
EX, EY, EZ = 32, 32, 128
TILES = 1024
SIDES = (("gx", 1), ("gx", -1), ("gy", 1), ("gy", -1), ("gz", 1), ("gz", -1))
FACE_SHAPES = ((EY, EZ), (EY, EZ), (EX, EZ), (EX, EZ), (EY, EX), (EY, EX))
VMEM = pltpu.MemorySpace.VMEM
SMEM = pltpu.MemorySpace.SMEM


def swap_blocks(t):
    row = lax.broadcasted_iota(jnp.int32, t.shape, 0)
    lane = lax.broadcasted_iota(jnp.int32, t.shape, 1)
    for k in range(4):
        s = 1 << k
        row_bit = (row >> k) & 1
        lane_bit = (lane >> (3 + k)) & 1
        a = pltpu.roll(pltpu.roll(t, 128 - s, 0), 8 * s, 1)
        b = pltpu.roll(pltpu.roll(t, s, 0), 128 - 8 * s, 1)
        t = jnp.where(row_bit == lane_bit, t, jnp.where(row_bit == 0, a, b))
    return t


def pack_kernel(flat_ref, tile_ref, sums_ref, out_ref):
    owners = out_ref.shape[0]
    rows = owners * 8
    row = lax.broadcasted_iota(jnp.int32, (rows, 128), 0)
    key = (row >> 3) * 4 + (row & 3)
    pick = (key == flat_ref[...]).astype(jnp.float32)
    low = (row & 7) < 4

    def take(values):
        return jnp.dot(
            pick, values, precision=lax.Precision.HIGHEST, preferred_element_type=jnp.float32
        )

    top = jnp.where(low, take(sums_ref[0]), take(sums_ref[1]))
    bottom = jnp.where(low, take(sums_ref[2]), take(tile_ref[...]))
    out_ref[:, 0:8, :] = top.reshape(owners, 8, 128)
    out_ref[:, 8:16, :] = bottom.reshape(owners, 8, 128)


def put_faces(read, faces, index):
    lane = lax.broadcasted_iota(jnp.int32, (EY, EX), 1)
    low = jnp.zeros((EY, EX), jnp.float32)
    high = jnp.zeros((EY, EX), jnp.float32)
    for x in range(EX):
        plane = read(x)
        low = jnp.where(lane == x, plane[:, 0:1], low)
        high = jnp.where(lane == x, plane[:, EZ - 1 : EZ], high)
        if x == 0:
            faces[1][index] = plane
        if x == EX - 1:
            faces[0][index] = plane
        faces[3][index, x : x + 1, :] = plane[0:1]
        faces[2][index, x : x + 1, :] = plane[EY - 1 : EY]
    faces[5][index] = low
    faces[4][index] = high


def grid_kernel(tile_ref, inc_ref, vel_ref, visc_ref, rhs_ref, *rest):
    faces, (acc_ref,) = rest[:6], rest[6:]
    acc_ref[...] = jnp.zeros_like(acc_ref)

    def add(owner, carry):
        for slot in range(4):
            tile = tile_ref[owner * 4 + slot]
            for c in range(3):
                acc_ref[c, pl.ds(tile, 1), :] += inc_ref[owner, 4 * c + slot : 4 * c + slot + 1, :]
        return carry

    lax.fori_loop(0, inc_ref.shape[0], add, 0)

    def spread(tx, carry):
        rows = pl.ds(pl.multiple_of(tx * 128, 128), 128)
        visc = jnp.exp(acc_ref[1, rows, :] / (1.0 + acc_ref[0, rows, :]))
        for values, out in ((visc, visc_ref), (acc_ref[2, rows, :], rhs_ref)):
            values = swap_blocks(values)
            for ty in range(8):
                for cx in range(4):
                    start = ty * 16 + cx * 4
                    out[tx * 4 + cx, ty * 4 : ty * 4 + 4, :] = values[start : start + 4]
        return carry

    lax.fori_loop(0, 8, spread, 0)
    put_faces(lambda x: visc_ref[x], faces, 0)
    put_faces(lambda x: vel_ref[x], faces, 1)


def sweep_kernel(first, last, coef_ref, field_ref, rhs_ref, visc_ref, *rest):
    visc_faces, rest = rest[:6], rest[6:]
    if first:
        field_faces, field_index = visc_faces, 1
    else:
        field_faces, rest = rest[:6], rest[6:]
        field_index = 0
        old_ref, rest = rest[0], rest[1:]
    out_ref, rest = rest[0], rest[1:]
    row = lax.broadcasted_iota(jnp.int32, (EY, EZ), 0)
    lane = lax.broadcasted_iota(jnp.int32, (EY, EZ), 1)

    def around(ref, faces, index, x):
        plane = ref[x]
        return (
            ref[x - 1] if x > 0 else faces[0][index],
            ref[x + 1] if x < EX - 1 else faces[1][index],
            jnp.where(row == 0, faces[2][index, x : x + 1, :], pltpu.roll(plane, 1, 0)),
            jnp.where(row == EY - 1, faces[3][index, x : x + 1, :], pltpu.roll(plane, EY - 1, 0)),
            jnp.where(lane == 0, faces[4][index, :, x : x + 1], pltpu.roll(plane, 1, 1)),
            jnp.where(lane == EZ - 1, faces[5][index, :, x : x + 1], pltpu.roll(plane, EZ - 1, 1)),
        )

    for x in range(EX):
        field = field_ref[x]
        visc = visc_ref[x]
        flux = jnp.zeros_like(field)
        diagonal = jnp.zeros_like(field)
        for near_visc, near_field in zip(
            around(visc_ref, visc_faces, 0, x), around(field_ref, field_faces, field_index, x)
        ):
            face = 0.5 * (visc + near_visc)
            diagonal = diagonal + face
            flux = flux + face * (field - near_field)
        update = coef_ref[1] * ((rhs_ref[x] - flux) / diagonal)
        if not first:
            update = coef_ref[0] * old_ref[x] + update
        out_ref[x] = field + update
        if not last:
            rest[0][x] = update
    if not last:
        put_faces(lambda x: out_ref[x], rest[1:7], 0)
        return
    tiles_ref, buffer = rest

    def gather(tx, carry):
        for ty in range(8):
            for cx in range(4):
                start = ty * 16 + cx * 4
                buffer[start : start + 4, :] = out_ref[tx * 4 + cx, ty * 4 : ty * 4 + 4, :]
        tiles_ref[pl.ds(pl.multiple_of(tx * 128, 128), 128), :] = swap_blocks(buffer[...])
        return carry

    lax.fori_loop(0, 8, gather, 0)


def call(kernel, outs, specs, args, scratch=()):
    return pl.pallas_call(
        kernel,
        out_shape=[jax.ShapeDtypeStruct(s, jnp.float32) for s in outs],
        in_specs=[pl.BlockSpec(memory_space=s) for s in specs],
        out_specs=[pl.BlockSpec(memory_space=VMEM)] * len(outs),
        scratch_shapes=[pltpu.VMEM(s, jnp.float32) for s in scratch],
        compiler_params=pltpu.CompilerParams(vmem_limit_bytes=40 * 1024 * 1024),
    )(*args)


def exchange(faces):
    received = []
    for face, (axis, step) in zip(faces, SIDES):
        ends = lax.axis_size(axis) - 1
        if step == 1:
            pairs = [(i, i + 1) for i in range(ends)]
        else:
            pairs = [(i + 1, i) for i in range(ends)]
        received.append(lax.ppermute(face, axis, pairs))
    return received


def smooth(velocity, rhs, viscosity, faces, low, high):
    centre = (high + low) / 2
    half_width = (high - low) / 2
    sigma_ratio = centre / half_width
    rho_now = 1.0 / sigma_ratio
    grid = (EX, EY, EZ)
    visc_faces = exchange(faces)
    field, update, field_faces = velocity, None, None
    for index in range(SWEEPS):
        first, last = index == 0, index == SWEEPS - 1
        args = [field, rhs, viscosity, *visc_faces]
        if first:
            coef = jnp.stack([jnp.zeros_like(centre), 1.0 / centre])
        else:
            rho_next = 1.0 / (2.0 * sigma_ratio - rho_now)
            coef = jnp.stack([rho_next * rho_now, 2.0 * rho_next / half_width])
            rho_now = rho_next
            args += [*field_faces, update]
        outs = [grid, (TILES, 128)] if last else [grid, grid] + [(1, *s) for s in FACE_SHAPES]
        results = call(
            functools.partial(sweep_kernel, first, last),
            outs,
            [SMEM] + [VMEM] * len(args),
            [coef, *args],
            [(128, 128)] if last else [],
        )
        if last:
            return results
        field, update = results[:2]
        field_faces = exchange(results[2:])


def one_hot_cells(cells):
    return (cells[..., None] == jnp.arange(TILE_CELLS, dtype=jnp.int32)).astype(jnp.float32)


def body(
    velocity,
    marker_logvisc,
    marker_force,
    marker_weight,
    marker_cell,
    block_count,
    block_owner,
    block_tile,
    eig_low,
    eig_high,
):
    blocks, slots = marker_weight.shape
    owners = lax.axis_size("gy") * lax.axis_size("gz")
    capacity = 4
    group = math.gcd(blocks, 64)
    groups = blocks // group
    live = jnp.arange(slots, dtype=jnp.int32)[None, :] < block_count[:, None]
    weight = jnp.where(live, marker_weight, 0.0)
    channels = jnp.stack([weight, weight * marker_logvisc, weight * marker_force])
    channels = channels.reshape(3, groups, group, slots).transpose(1, 0, 2, 3)
    cells_grouped = marker_cell.reshape(groups, group, slots)

    def project(pair):
        cells, values = pair
        return jnp.einsum(
            "gsk,cgs->gck", one_hot_cells(cells), values, precision=lax.Precision.HIGHEST
        )

    block_sums = lax.map(project, (cells_grouped, channels)).reshape(blocks, 3, TILE_CELLS)
    block_sums = block_sums.transpose(1, 0, 2)
    owner = block_owner[:, 0]
    member = (owner[:, None] == jnp.arange(owners, dtype=jnp.int32)[None, :]).astype(jnp.int32)
    slot_of = jnp.sum(jnp.cumsum(member, axis=0) * member, axis=1) - 1
    flat = owner * capacity + slot_of
    tile_wide = jnp.broadcast_to(block_tile.astype(jnp.float32)[:, None], (blocks, 128))
    (outgoing,) = call(
        pack_kernel, [(owners, 16, 128)], [VMEM] * 3, [flat[None, :], tile_wide, block_sums]
    )
    incoming = lax.all_to_all(outgoing, ("gy", "gz"), split_axis=0, concat_axis=0, tiled=True)
    tile_in = incoming[:, 12:16, 0].astype(jnp.int32).reshape(owners * capacity)
    results = call(
        grid_kernel,
        [(EX, EY, EZ)] * 2 + [(2, *s) for s in FACE_SHAPES],
        [SMEM, VMEM, VMEM],
        [tile_in, incoming, velocity],
        [(3, TILES, 128)],
    )
    viscosity, rhs = results[:2]
    smoothed, tile_view = smooth(velocity, rhs, viscosity, results[2:], eig_low[0], eig_high[0])
    returning = tile_view[tile_in].reshape(owners, capacity, TILE_CELLS)
    arrived = lax.all_to_all(returning, ("gy", "gz"), split_axis=0, concat_axis=0, tiled=True)
    block_values = arrived[owner, slot_of].reshape(groups, group, TILE_CELLS)

    def interpolate(pair):
        cells, values = pair
        return jnp.einsum(
            "gsk,gk->gs", one_hot_cells(cells), values, precision=lax.Precision.HIGHEST
        )

    picked = lax.map(interpolate, (cells_grouped, block_values)).reshape(blocks, slots)
    marker_velocity = jnp.where(live, picked, 0.0)
    return (smoothed, marker_velocity)


def solution(mesh):
    return jax.shard_map(
        body,
        mesh=mesh,
        in_specs=(
            P("gx", "gy", "gz"),
            P(("gx", "gy", "gz"), None),
            P(("gx", "gy", "gz"), None),
            P(("gx", "gy", "gz"), None),
            P(("gx", "gy", "gz"), None),
            P(("gx", "gy", "gz")),
            P(("gx", "gy", "gz"), None),
            P(("gx", "gy", "gz")),
            P(),
            P(),
        ),
        out_specs=(P("gx", "gy", "gz"), P(("gx", "gy", "gz"), None)),
        check_vma=False,
    )
```

time: 305 us -> 168 us (0.55)
  local copies, waits for them, and re-layouts: 101 us -> 2.74 us
  starting transfers between devices: 118 us -> 76.4 us
  blocking collectives: 0 us -> 32.8 us
  other arithmetic: 36.2 us -> 6.39 us
  Pallas kernels: 0 us -> 17.6 us
  waiting for transfers between devices: 30.5 us -> 14.5 us
    all_to_all x0 -> x1, blocking collectives: none -> 32.8 us  [body(): lax.all_to_all(outgoing, ('gy', 'gz'), split_axis=0, concat_axis=0, tiled...]
    all_to_all x2 -> x0, starting transfers between devices: 26 us -> none  [the longest x1 14.8 us: body(): lax.all_to_all(tile_out, ('gy', 'gz'), split_axis=0, concat_axis=0, tiled...]
    slice x19 -> x0, local copies, waits for them, and re-layouts: 19.1 us -> none  [the longest x10 7.23 us: with_halo(): head = lax.slice_in_dim(cells, 0, width, axis=dim)]
    reshape x4 -> x0, local copies, waits for them, and re-layouts: 19 us -> none  [the longest x1 7.06 us: body(): tile_acc.reshape(tiles_x, tiles_y, tiles_z, 3, TILE_X, TILE_Y, TILE_Z)]
    pallas_call x0 -> x5, Pallas kernels: none -> 17.6 us  [call(): pl.pallas_call(kernel, out_shape=[jax.ShapeDtypeStruct(s, jnp.float32) fo...]
    scatter x3 -> x0, local copies, waits for them, and re-layouts: 17.5 us -> none  [the longest x1 11 us: body(): jnp.zeros((owners, capacity), jnp.int32).at[owner, slot_of].set(block_tile)]
    ppermute x24 -> x18, waiting for transfers between devices: 19.9 us -> 3.98 us  [exchange(): received.append(lax.ppermute(face, axis, pairs))]
    add x3 -> x1, other arithmetic: 16 us -> 0.67 us  [body(): flat = owner * capacity + slot_of]
  transfers between devices with their start and end apart: 27 -> 19, of which waited for: 8 -> 4; matrix products, arithmetic and copies ran while one was open for 25% -> 0% of each run, Pallas kernels for 0% -> 0%
where the time goes in v1:
time: 168 us; the launch traced here: 167 us
  starting transfers between devices  76.4 us (45%)
  blocking collectives  32.8 us (20%)
  Pallas kernels  17.6 us (10%)
  waiting for transfers between devices  14.5 us (9%)
  matrix products  13.8 us (8%)
  other arithmetic  6.39 us (4%)
  local copies, waits for them, and re-layouts  2.74 us (2%)
  between operations  2.63 us (2%)
    ppermute x18, starting transfers between devices, exchange(): received.append(lax.ppermute(face, axis, pairs))  63.1 us
    all_to_all x1, blocking collectives, body(): lax.all_to_all(outgoing, ('gy', 'gz'), split_axis=0, concat_axis=0, tiled...  32.8 us
    pallas_call x5, Pallas kernels, call(): pl.pallas_call(kernel, out_shape=[jax.ShapeDtypeStruct(s, jnp.float32) fo...  17.6 us
    all_to_all x1, starting transfers between devices, body(): lax.all_to_all(returning, ('gy', 'gz'), split_axis=0, concat_axis=0, tile...  13.3 us
    all_to_all x1, waiting for transfers between devices, body(): lax.all_to_all(returning, ('gy', 'gz'), split_axis=0, concat_axis=0, tile...  10.6 us
    dot_general x2, matrix products, interpolate(): jnp.einsum('gsk,gk->gs', one_hot_cells(cells), values, precision=lax.Prec...  7.99 us
    dot_general x2, matrix products, project(): jnp.einsum('gsk,cgs->gck', one_hot_cells(cells), values, precision=lax.Pr...  5.84 us
    ppermute x18, waiting for transfers between devices, exchange(): received.append(lax.ppermute(face, axis, pairs))  3.98 us
  transfers between devices with their start and end apart: 19, of which 4 were waited for; matrix products, arithmetic and copies ran while one was open for 0% of the time, Pallas kernels for 0%

profile of v1, /device:TPU:40, one launch (start us, length us, event | category | flops | bytes accessed | tf_op | source)
XLA Modules:
  0.0 167.1 jit_solution(10149125643857221703)
XLA Ops:
  0.6 0.8 fusion.10
  1.4 0.2 reduce_window_sum.11
  1.6 0.9 select_reduce_fusion
  2.5 0.7 bitcast_add_fusion.flat_ref
  3.1 0.7 convert_element_type.26
  3.8 1.0 fusion.16
  4.8 0.2 maximum_bitcast_fusion
  5.0 6.0 %while.20 = (s32[]{:T(128)}, f32[2,64,3,128]{3,1,0,2:T(8,128)S(1)}, f32[2,3,64,128]{3,1,2,0:T(4,128)S(1)}, s32[2,64,128]{2,1,0:T(8,128)S(1)}, s32[]{:T(128)}) while((s32[]{:T(128)}, f32[2,64,3,128]{3,1,0,2:T(8,128)S(1)}, f32[2,3,64,128]{3,1,2,0:T(4,128)S(1)}, s32[2,64,128]{2,1,0:T(8,128)S(1)}, s32[]{:T(128)}) %tuple.42), condition=%wide.region_3.4_spmd, body=%wide.region_2.3_spmd.sunk | while | flops 38797312 | bytes 557137 | solution.py:244
  5.0 2.9 %fusion.24 = f32[1,64,3,128]{3,2,1,0:T(4,128)S(1)} fusion(s32[64,128]{1,0:T(8,128)S(1)} %dynamic-slice_bitcast_fusion.4, f32[2,3,64,128]{3,1,2,0:T(4,128)S(1)} %get-tuple-element.180, s32[]{:T(128)S(6)} %copy.31), kind=kOutput, calls=%fused_computation.5.clone.1 | convolution fusion | flops 38797312 | bytes 262148 | tf_op jit(solution)/shard_map/while/body/eval_jaxpr/gsk,cgs->gck/dot_general | solution.py:240
  8.0 2.9 %fusion.24 = f32[1,64,3,128]{3,2,1,0:T(4,128)S(1)} fusion(s32[64,128]{1,0:T(8,128)S(1)} %dynamic-slice_bitcast_fusion.4, f32[2,3,64,128]{3,1,2,0:T(4,128)S(1)} %get-tuple-element.180, s32[]{:T(128)S(6)} %copy.31), kind=kOutput, calls=%fused_computation.5.clone.1 | convolution fusion | flops 38797312 | bytes 262148 | tf_op jit(solution)/shard_map/while/body/eval_jaxpr/gsk,cgs->gck/dot_general | solution.py:240
  11.0 1.0 shard_map.113
  12.1 32.8 %all_to_all.10.inc_ref = f32[64,16,128]{2,1,0:T(8,128)S(1)} all-to-all(f32[64,16,128]{2,1,0:T(8,128)S(1)} %shard_map.113), channel_id=1, replica_groups=mesh['gx'=8,'gy'=8,'gz'=8] {'gy','gz'}, dimensions={0} | all-to-all | bytes 1048576 | tf_op jit(solution)/shard_map/all_to_all | solution.py:254
  44.9 1.2 fusion.8
  46.1 0.1 convert_element_type.28.tile_ref
  46.2 6.8 %shard_map.114 = (f32[32,32,128]{2,1,0:T(8,128)S(1)}, f32[32,32,128]{2,1,0:T(8,128)S(1)}, f32[2,32,128]{2,1,0:T(8,128)S(1)}, f32[2,32,128]{2,1,0:T(8,128)S(1)}, ...) custom-call(s32[256]{0:T(256)S(1)} %convert_element_type.28.tile_ref, ...), custom_call_target="tpu_custom_call" | custom-call | tf_op jit(solution)/shard_map/pallas_call | solution.py:157
  53.0 2.2 %collective-permute-start.4 = (f32[2,32,32]{2,1,0:T(8,128)S(1)}, f32[2,32,32]{2,1,0:T(8,128)S(1)}, u32[]{:S(2)}, u32[]{:S(2)}) collective-permute-start(f32[2,32,32]{2,1,0:T(8,128)S(1)} %get-tuple-element.79), channel_id=1, source_target_pairs={{0,1},{1,2},{2,3},{3,4},{4,5},{5,6},{6,7},{8,9},{9,10},{10,11},{11... | collective-permute-start | bytes 24584 | tf_op jit(solution)/shard_map/ppermute | solution.py:175
  56.5 1.9 %collective-permute-start = (f32[2,32,128]{2,1,0:T(8,128)S(1)}, f32[2,32,128]{2,1,0:T(8,128)S(1)}, u32[]{:S(2)}, u32[]{:S(2)}) collective-permute-start(f32[2,32,128]{2,1,0:T(8,128)S(1)} %get-tuple-element.75), channel_id=1, source_target_pairs={{0,64},{64,128},{128,192},{192,256},{256,320},{320,384},{384,448},... | collective-permute-start | bytes 98312 | tf_op jit(solution)/shard_map/ppermute | solution.py:175
  58.5 5.8 %collective-permute-start.1 = (f32[2,32,128]{2,1,0:T(8,128)S(1)}, f32[2,32,128]{2,1,0:T(8,128)S(1)}, u32[]{:S(2)}, u32[]{:S(2)}) collective-permute-start(f32[2,32,128]{2,1,0:T(8,128)S(1)} %get-tuple-element.76), channel_id=1, source_target_pairs={{64,0},{128,64},{192,128},{256,192},{320,256},{384,320},{448,384},... | collective-permute-start | bytes 98312 | tf_op jit(solution)/shard_map/ppermute | solution.py:175
  64.2 3.4 %collective-permute-start.2 = (f32[2,32,128]{2,1,0:T(8,128)S(1)}, f32[2,32,128]{2,1,0:T(8,128)S(1)}, u32[]{:S(2)}, u32[]{:S(2)}) collective-permute-start(f32[2,32,128]{2,1,0:T(8,128)S(1)} %get-tuple-element.77), channel_id=1, source_target_pairs={{0,8},{8,16},{16,24},{24,32},{32,40},{40,48},{48,56},{1,9},{9,17},... | collective-permute-start | bytes 98312 | tf_op jit(solution)/shard_map/ppermute | solution.py:175
  67.7 1.3 collective-permute-start.3
  69.0 5.0 %collective-permute-start.5 = (f32[2,32,32]{2,1,0:T(8,128)S(1)}, f32[2,32,32]{2,1,0:T(8,128)S(1)}, u32[]{:S(2)}, u32[]{:S(2)}) collective-permute-start(f32[2,32,32]{2,1,0:T(8,128)S(1)} %get-tuple-element.80), channel_id=1, source_target_pairs={{1,0},{2,1},{3,2},{4,3},{5,4},{6,5},{7,6},{9,8},{10,9},{11,10},{12... | collective-permute-start | bytes 24584 | tf_op jit(solution)/shard_map/ppermute | solution.py:175
  74.3 1.3 collective-permute-done.5.rest_5_
  75.6 2.3 %shard_map.115 = (f32[32,32,128]{2,1,0:T(8,128)S(1)}, f32[32,32,128]{2,1,0:T(8,128)S(1)}, f32[1,32,128]{2,1,0:T(8,128)S(1)}, f32[1,32,128]{2,1,0:T(8,128)S(1)}, ...) custom-call(f32[2]{0:T(128)S(1)} %pad_maximum_fusion.2.coef_ref, ...), custom_call_target="tpu_custom_call" | custom-call | tf_op jit(solution)/shard_map/pallas_call | solution.py:157
  77.9 2.0 %collective-permute-start.10 = (f32[1,32,32]{2,1,0:T(8,128)S(1)}, f32[1,32,32]{2,1,0:T(8,128)S(1)}, u32[]{:S(2)}, u32[]{:S(2)}) collective-permute-start(f32[1,32,32]{2,1,0:T(8,128)S(1)} %get-tuple-element.86), channel_id=1, source_target_pairs={{0,1},{1,2},{2,3},{3,4},{4,5},{5,6},{6,7},{8,9},{9,10},{10,11},{11... | collective-permute-start | bytes 12296 | tf_op jit(solution)/shard_map/ppermute | solution.py:175
  80.0 1.9 %collective-permute-start.6 = (f32[1,32,128]{2,1,0:T(8,128)S(1)}, f32[1,32,128]{2,1,0:T(8,128)S(1)}, u32[]{:S(2)}, u32[]{:S(2)}) collective-permute-start(f32[1,32,128]{2,1,0:T(8,128)S(1)} %get-tuple-element.82), channel_id=1, source_target_pairs={{0,64},{64,128},{128,192},{192,256},{256,320},{320,384},{384,448},... | collective-permute-start | bytes 49160 | tf_op jit(solution)/shard_map/ppermute | solution.py:175
  81.9 5.8 %collective-permute-start.7 = (f32[1,32,128]{2,1,0:T(8,128)S(1)}, f32[1,32,128]{2,1,0:T(8,128)S(1)}, u32[]{:S(2)}, u32[]{:S(2)}) collective-permute-start(f32[1,32,128]{2,1,0:T(8,128)S(1)} %get-tuple-element.83), channel_id=1, source_target_pairs={{64,0},{128,64},{192,128},{256,192},{320,256},{384,320},{448,384},... | collective-permute-start | bytes 49160 | tf_op jit(solution)/shard_map/ppermute | solution.py:175
  87.7 4.5 %collective-permute-start.8 = (f32[1,32,128]{2,1,0:T(8,128)S(1)}, f32[1,32,128]{2,1,0:T(8,128)S(1)}, u32[]{:S(2)}, u32[]{:S(2)}) collective-permute-start(f32[1,32,128]{2,1,0:T(8,128)S(1)} %get-tuple-element.84), channel_id=1, source_target_pairs={{0,8},{8,16},{16,24},{24,32},{32,40},{40,48},{48,56},{1,9},{9,17},... | collective-permute-start | bytes 49160 | tf_op jit(solution)/shard_map/ppermute | solution.py:175
  92.2 1.3 collective-permute-start.9
  93.6 6.3 %collective-permute-start.11 = (f32[1,32,32]{2,1,0:T(8,128)S(1)}, f32[1,32,32]{2,1,0:T(8,128)S(1)}, u32[]{:S(2)}, u32[]{:S(2)}) collective-permute-start(f32[1,32,32]{2,1,0:T(8,128)S(1)} %get-tuple-element.87), channel_id=1, source_target_pairs={{1,0},{2,1},{3,2},{4,3},{5,4},{6,5},{7,6},{9,8},{10,9},{11,10},{12... | collective-permute-start | bytes 12296 | tf_op jit(solution)/shard_map/ppermute | solution.py:175
  99.9 0.1 convert_element_type.29
  100.0 1.2 collective-permute-done.11.rest_11_
  101.3 2.3 %shard_map.116 = (f32[32,32,128]{2,1,0:T(8,128)S(1)}, f32[32,32,128]{2,1,0:T(8,128)S(1)}, f32[1,32,128]{2,1,0:T(8,128)S(1)}, f32[1,32,128]{2,1,0:T(8,128)S(1)}, ...) custom-call(f32[2]{0:T(128)S(1)} %pad_maximum_fusion.1.coef_ref, ...), custom_call_target="tpu_custom_call" | custom-call | tf_op jit(solution)/shard_map/pallas_call | solution.py:157
  103.6 1.9 %collective-permute-start.16 = (f32[1,32,32]{2,1,0:T(8,128)S(1)}, f32[1,32,32]{2,1,0:T(8,128)S(1)}, u32[]{:S(2)}, u32[]{:S(2)}) collective-permute-start(f32[1,32,32]{2,1,0:T(8,128)S(1)} %get-tuple-element.94), channel_id=1, source_target_pairs={{0,1},{1,2},{2,3},{3,4},{4,5},{5,6},{6,7},{8,9},{9,10},{10,11},{11... | collective-permute-start | bytes 12296 | tf_op jit(solution)/shard_map/ppermute | solution.py:175
  105.5 1.9 %collective-permute-start.12 = (f32[1,32,128]{2,1,0:T(8,128)S(1)}, f32[1,32,128]{2,1,0:T(8,128)S(1)}, u32[]{:S(2)}, u32[]{:S(2)}) collective-permute-start(f32[1,32,128]{2,1,0:T(8,128)S(1)} %get-tuple-element.90), channel_id=1, source_target_pairs={{0,64},{64,128},{128,192},{192,256},{256,320},{320,384},{384,448},... | collective-permute-start | bytes 49160 | tf_op jit(solution)/shard_map/ppermute | solution.py:175
  107.5 5.8 %collective-permute-start.13 = (f32[1,32,128]{2,1,0:T(8,128)S(1)}, f32[1,32,128]{2,1,0:T(8,128)S(1)}, u32[]{:S(2)}, u32[]{:S(2)}) collective-permute-start(f32[1,32,128]{2,1,0:T(8,128)S(1)} %get-tuple-element.91), channel_id=1, source_target_pairs={{64,0},{128,64},{192,128},{256,192},{320,256},{384,320},{448,384},... | collective-permute-start | bytes 49160 | tf_op jit(solution)/shard_map/ppermute | solution.py:175
  113.2 4.5 %collective-permute-start.14 = (f32[1,32,128]{2,1,0:T(8,128)S(1)}, f32[1,32,128]{2,1,0:T(8,128)S(1)}, u32[]{:S(2)}, u32[]{:S(2)}) collective-permute-start(f32[1,32,128]{2,1,0:T(8,128)S(1)} %get-tuple-element.92), channel_id=1, source_target_pairs={{0,8},{8,16},{16,24},{24,32},{32,40},{40,48},{48,56},{1,9},{9,17},... | collective-permute-start | bytes 49160 | tf_op jit(solution)/shard_map/ppermute | solution.py:175
  117.8 1.3 collective-permute-start.15
  119.1 6.3 %collective-permute-start.17 = (f32[1,32,32]{2,1,0:T(8,128)S(1)}, f32[1,32,32]{2,1,0:T(8,128)S(1)}, u32[]{:S(2)}, u32[]{:S(2)}) collective-permute-start(f32[1,32,32]{2,1,0:T(8,128)S(1)} %get-tuple-element.95), channel_id=1, source_target_pairs={{1,0},{2,1},{3,2},{4,3},{5,4},{6,5},{7,6},{9,8},{10,9},{11,10},{12... | collective-permute-start | bytes 12296 | tf_op jit(solution)/shard_map/ppermute | solution.py:175
  125.4 1.4 collective-permute-done.17.rest_11_
  126.9 5.2 %shard_map.117 = (f32[32,32,128]{2,1,0:T(8,128)}, f32[1024,128]{1,0:T(8,128)S(1)}) custom-call(f32[2]{0:T(128)S(1)} %pad_maximum_fusion.coef_ref, f32[32,32,128]{2,1,0:T(8,128)S(1)} %get-tuple-element.89.field_ref, f32[32,32,128]{2,1,0:T(8,128)S(1)} %get-tuple-element.73.rhs_ref, f32[32,32,128]{2,1,0:T(8,128)S(1)} %get-tuple-element.74.visc_ref, ...), custom_call_target="tpu_custom_call" | custom-call | tf_op jit(solution)/shard_map/pallas_call | solution.py:157
  132.0 1.3 gather_fusion
  133.4 13.3 %all-to-all-start.1 = ((f32[64,4,128]{2,1,0:T(4,128)}), f32[64,4,128]{2,1,0:T(4,128)S(1)}, u32[]{:S(2)}, u32[]{:S(2)}) async-start(f32[64,4,128]{2,1,0:T(4,128)} %bitcast.31), calls=%async_computation.1 | async-start | bytes 262144 | tf_op jit(solution)/shard_map/all_to_all | solution.py:266
  146.7 10.6 %all-to-all-done.1 = f32[64,4,128]{2,1,0:T(4,128)S(1)} async-done(((f32[64,4,128]{2,1,0:T(4,128)}), f32[64,4,128]{2,1,0:T(4,128)S(1)}, u32[]{:S(2)}, u32[]{:S(2)}) %all-to-all-start.1) | async-done | bytes 131104 | tf_op jit(solution)/shard_map/all_to_all | solution.py:266
  157.3 1.0 gather_fusion.1
  158.3 8.1 %while.21 = (s32[]{:T(128)}, f32[2,64,128]{2,1,0:T(8,128)S(1)}, s32[2,64,128]{2,1,0:T(8,128)S(1)}, f32[2,64,128]{2,1,0:T(8,128)S(1)}, s32[]{:T(128)}) while((s32[]{:T(128)}, f32[2,64,128]{2,1,0:T(8,128)S(1)}, s32[2,64,128]{2,1,0:T(8,128)S(1)}, f32[2,64,128]{2,1,0:T(8,128)S(1)}, s32[]{:T(128)}) %tuple.44), condition=%wide.region_5.6_spmd, body=%wide.region_4.5_spmd.sunk | while | flops 13631490 | bytes 294993 | solution.py:275
  158.3 4.0 %fusion.26 = f32[64,1,128]{2,1,0:T(1,128)S(1)} fusion(f32[64,128,1]{1,2,0:T(1,128)S(1)} %bitcast.81, s32[64,128]{1,0:T(8,128)S(1)} %dynamic-slice_bitcast_fusion.5), kind=kOutput, calls=%fused_computation.12.clone.1 | convolution fusion | flops 13631488 | bytes 98304 | tf_op jit(solution)/shard_map/while/body/eval_jaxpr/gsk,gk->gs/dot_general | solution.py:271
  162.4 4.0 %fusion.26 = f32[64,1,128]{2,1,0:T(1,128)S(1)} fusion(f32[64,128,1]{1,2,0:T(1,128)S(1)} %bitcast.81, s32[64,128]{1,0:T(8,128)S(1)} %dynamic-slice_bitcast_fusion.5), kind=kOutput, calls=%fused_computation.12.clone.1 | convolution fusion | flops 13631488 | bytes 98304 | tf_op jit(solution)/shard_map/while/body/eval_jaxpr/gsk,gk->gs/dot_general | solution.py:271
  166.4 0.7 bitcast_select_fusion
  (45 shorter events, 0.5 us)
Async XLA Ops:
  0.6 4.1 %copy-start.2 = (f32[128,128]{1,0:T(8,128)S(1)}, f32[128,128]{1,0:T(8,128)}, u32[]{:S(2)}) copy-start(f32[128,128]{1,0:T(8,128)} %param.16) | copy-start | bytes 196612
  1.6 3.4 %copy-start.1 = (s32[128,128]{1,0:T(8,128)S(1)}, s32[128,128]{1,0:T(8,128)}, u32[]{:S(2)}) copy-start(s32[128,128]{1,0:T(8,128)} %param.18) | copy-start | bytes 196612
  12.0 34.1 %copy-start = (f32[32,32,128]{2,1,0:T(8,128)S(1)}, f32[32,32,128]{2,1,0:T(8,128)}, u32[]{:S(2)}) copy-start(f32[32,32,128]{2,1,0:T(8,128)} %field_ref.1) | copy-start | bytes 1572868
  53.0 16.0 %collective-permute-start.4 = (f32[2,32,32]{2,1,0:T(8,128)S(1)}, f32[2,32,32]{2,1,0:T(8,128)S(1)}, u32[]{:S(2)}, u32[]{:S(2)}) collective-permute-start(f32[2,32,32]{2,1,0:T(8,128)S(1)} %get-tuple-element.79), channel_id=1, source_target_pairs={{0,1},{1,2},{2,3},{3,4},{4,5},{5,6},{6,7},{8,9},{9,10},{10,11},{11... | collective-permute-start | bytes 24584 | tf_op jit(solution)/shard_map/ppermute | solution.py:175
  56.5 19.0 %collective-permute-start = (f32[2,32,128]{2,1,0:T(8,128)S(1)}, f32[2,32,128]{2,1,0:T(8,128)S(1)}, u32[]{:S(2)}, u32[]{:S(2)}) collective-permute-start(f32[2,32,128]{2,1,0:T(8,128)S(1)} %get-tuple-element.75), channel_id=1, source_target_pairs={{0,64},{64,128},{128,192},{192,256},{256,320},{320,384},{384,448},... | collective-permute-start | bytes 98312 | tf_op jit(solution)/shard_map/ppermute | solution.py:175
  58.5 17.1 %collective-permute-start.1 = (f32[2,32,128]{2,1,0:T(8,128)S(1)}, f32[2,32,128]{2,1,0:T(8,128)S(1)}, u32[]{:S(2)}, u32[]{:S(2)}) collective-permute-start(f32[2,32,128]{2,1,0:T(8,128)S(1)} %get-tuple-element.76), channel_id=1, source_target_pairs={{64,0},{128,64},{192,128},{256,192},{320,256},{384,320},{448,384},... | collective-permute-start | bytes 98312 | tf_op jit(solution)/shard_map/ppermute | solution.py:175
  64.2 11.4 %collective-permute-start.2 = (f32[2,32,128]{2,1,0:T(8,128)S(1)}, f32[2,32,128]{2,1,0:T(8,128)S(1)}, u32[]{:S(2)}, u32[]{:S(2)}) collective-permute-start(f32[2,32,128]{2,1,0:T(8,128)S(1)} %get-tuple-element.77), channel_id=1, source_target_pairs={{0,8},{8,16},{16,24},{24,32},{32,40},{40,48},{48,56},{1,9},{9,17},... | collective-permute-start | bytes 98312 | tf_op jit(solution)/shard_map/ppermute | solution.py:175
  67.7 7.9 %collective-permute-start.3 = (f32[2,32,128]{2,1,0:T(8,128)S(1)}, f32[2,32,128]{2,1,0:T(8,128)S(1)}, u32[]{:S(2)}, u32[]{:S(2)}) collective-permute-start(f32[2,32,128]{2,1,0:T(8,128)S(1)} %get-tuple-element.78), channel_id=1, source_target_pairs={{8,0},{16,8},{24,16},{32,24},{40,32},{48,40},{56,48},{9,1},{17,9},... | collective-permute-start | bytes 98312 | tf_op jit(solution)/shard_map/ppermute | solution.py:175
  69.0 6.6 %collective-permute-start.5 = (f32[2,32,32]{2,1,0:T(8,128)S(1)}, f32[2,32,32]{2,1,0:T(8,128)S(1)}, u32[]{:S(2)}, u32[]{:S(2)}) collective-permute-start(f32[2,32,32]{2,1,0:T(8,128)S(1)} %get-tuple-element.80), channel_id=1, source_target_pairs={{1,0},{2,1},{3,2},{4,3},{5,4},{6,5},{7,6},{9,8},{10,9},{11,10},{12... | collective-permute-start | bytes 24584 | tf_op jit(solution)/shard_map/ppermute | solution.py:175
  77.9 15.6 %collective-permute-start.10 = (f32[1,32,32]{2,1,0:T(8,128)S(1)}, f32[1,32,32]{2,1,0:T(8,128)S(1)}, u32[]{:S(2)}, u32[]{:S(2)}) collective-permute-start(f32[1,32,32]{2,1,0:T(8,128)S(1)} %get-tuple-element.86), channel_id=1, source_target_pairs={{0,1},{1,2},{2,3},{3,4},{4,5},{5,6},{6,7},{8,9},{9,10},{10,11},{11... | collective-permute-start | bytes 12296 | tf_op jit(solution)/shard_map/ppermute | solution.py:175
  80.0 21.3 %collective-permute-start.6 = (f32[1,32,128]{2,1,0:T(8,128)S(1)}, f32[1,32,128]{2,1,0:T(8,128)S(1)}, u32[]{:S(2)}, u32[]{:S(2)}) collective-permute-start(f32[1,32,128]{2,1,0:T(8,128)S(1)} %get-tuple-element.82), channel_id=1, source_target_pairs={{0,64},{64,128},{128,192},{192,256},{256,320},{320,384},{384,448},... | collective-permute-start | bytes 49160 | tf_op jit(solution)/shard_map/ppermute | solution.py:175
  81.9 19.3 %collective-permute-start.7 = (f32[1,32,128]{2,1,0:T(8,128)S(1)}, f32[1,32,128]{2,1,0:T(8,128)S(1)}, u32[]{:S(2)}, u32[]{:S(2)}) collective-permute-start(f32[1,32,128]{2,1,0:T(8,128)S(1)} %get-tuple-element.83), channel_id=1, source_target_pairs={{64,0},{128,64},{192,128},{256,192},{320,256},{384,320},{448,384},... | collective-permute-start | bytes 49160 | tf_op jit(solution)/shard_map/ppermute | solution.py:175
  87.7 13.6 %collective-permute-start.8 = (f32[1,32,128]{2,1,0:T(8,128)S(1)}, f32[1,32,128]{2,1,0:T(8,128)S(1)}, u32[]{:S(2)}, u32[]{:S(2)}) collective-permute-start(f32[1,32,128]{2,1,0:T(8,128)S(1)} %get-tuple-element.84), channel_id=1, source_target_pairs={{0,8},{8,16},{16,24},{24,32},{32,40},{40,48},{48,56},{1,9},{9,17},... | collective-permute-start | bytes 49160 | tf_op jit(solution)/shard_map/ppermute | solution.py:175
  92.2 9.0 %collective-permute-start.9 = (f32[1,32,128]{2,1,0:T(8,128)S(1)}, f32[1,32,128]{2,1,0:T(8,128)S(1)}, u32[]{:S(2)}, u32[]{:S(2)}) collective-permute-start(f32[1,32,128]{2,1,0:T(8,128)S(1)} %get-tuple-element.85), channel_id=1, source_target_pairs={{8,0},{16,8},{24,16},{32,24},{40,32},{48,40},{56,48},{9,1},{17,9},... | collective-permute-start | bytes 49160 | tf_op jit(solution)/shard_map/ppermute | solution.py:175
  93.6 7.7 %collective-permute-start.11 = (f32[1,32,32]{2,1,0:T(8,128)S(1)}, f32[1,32,32]{2,1,0:T(8,128)S(1)}, u32[]{:S(2)}, u32[]{:S(2)}) collective-permute-start(f32[1,32,32]{2,1,0:T(8,128)S(1)} %get-tuple-element.87), channel_id=1, source_target_pairs={{1,0},{2,1},{3,2},{4,3},{5,4},{6,5},{7,6},{9,8},{10,9},{11,10},{12... | collective-permute-start | bytes 12296 | tf_op jit(solution)/shard_map/ppermute | solution.py:175
  103.6 15.5 %collective-permute-start.16 = (f32[1,32,32]{2,1,0:T(8,128)S(1)}, f32[1,32,32]{2,1,0:T(8,128)S(1)}, u32[]{:S(2)}, u32[]{:S(2)}) collective-permute-start(f32[1,32,32]{2,1,0:T(8,128)S(1)} %get-tuple-element.94), channel_id=1, source_target_pairs={{0,1},{1,2},{2,3},{3,4},{4,5},{5,6},{6,7},{8,9},{9,10},{10,11},{11... | collective-permute-start | bytes 12296 | tf_op jit(solution)/shard_map/ppermute | solution.py:175
  105.5 21.3 %collective-permute-start.12 = (f32[1,32,128]{2,1,0:T(8,128)S(1)}, f32[1,32,128]{2,1,0:T(8,128)S(1)}, u32[]{:S(2)}, u32[]{:S(2)}) collective-permute-start(f32[1,32,128]{2,1,0:T(8,128)S(1)} %get-tuple-element.90), channel_id=1, source_target_pairs={{0,64},{64,128},{128,192},{192,256},{256,320},{320,384},{384,448},... | collective-permute-start | bytes 49160 | tf_op jit(solution)/shard_map/ppermute | solution.py:175
  107.5 19.4 %collective-permute-start.13 = (f32[1,32,128]{2,1,0:T(8,128)S(1)}, f32[1,32,128]{2,1,0:T(8,128)S(1)}, u32[]{:S(2)}, u32[]{:S(2)}) collective-permute-start(f32[1,32,128]{2,1,0:T(8,128)S(1)} %get-tuple-element.91), channel_id=1, source_target_pairs={{64,0},{128,64},{192,128},{256,192},{320,256},{384,320},{448,384},... | collective-permute-start | bytes 49160 | tf_op jit(solution)/shard_map/ppermute | solution.py:175
  113.2 13.6 %collective-permute-start.14 = (f32[1,32,128]{2,1,0:T(8,128)S(1)}, f32[1,32,128]{2,1,0:T(8,128)S(1)}, u32[]{:S(2)}, u32[]{:S(2)}) collective-permute-start(f32[1,32,128]{2,1,0:T(8,128)S(1)} %get-tuple-element.92), channel_id=1, source_target_pairs={{0,8},{8,16},{16,24},{24,32},{32,40},{40,48},{48,56},{1,9},{9,17},... | collective-permute-start | bytes 49160 | tf_op jit(solution)/shard_map/ppermute | solution.py:175
  117.8 9.1 %collective-permute-start.15 = (f32[1,32,128]{2,1,0:T(8,128)S(1)}, f32[1,32,128]{2,1,0:T(8,128)S(1)}, u32[]{:S(2)}, u32[]{:S(2)}) collective-permute-start(f32[1,32,128]{2,1,0:T(8,128)S(1)} %get-tuple-element.93), channel_id=1, source_target_pairs={{8,0},{16,8},{24,16},{32,24},{40,32},{48,40},{56,48},{9,1},{17,9},... | collective-permute-start | bytes 49160 | tf_op jit(solution)/shard_map/ppermute | solution.py:175
  119.1 7.7 %collective-permute-start.17 = (f32[1,32,32]{2,1,0:T(8,128)S(1)}, f32[1,32,32]{2,1,0:T(8,128)S(1)}, u32[]{:S(2)}, u32[]{:S(2)}) collective-permute-start(f32[1,32,32]{2,1,0:T(8,128)S(1)} %get-tuple-element.95), channel_id=1, source_target_pairs={{1,0},{2,1},{3,2},{4,3},{5,4},{6,5},{7,6},{9,8},{10,9},{11,10},{12... | collective-permute-start | bytes 12296 | tf_op jit(solution)/shard_map/ppermute | solution.py:175
  132.0 14.6 %copy-start.3 = (s32[128,1]{0,1:T(1,128)S(1)}, s32[128,1]{0,1:T(1,128)}, u32[]{:S(2)}) copy-start(s32[128,1]{0,1:T(1,128)} %param.20) | copy-start | bytes 1540
  133.4 23.9 %all-to-all-start.1 = ((f32[64,4,128]{2,1,0:T(4,128)}), f32[64,4,128]{2,1,0:T(4,128)S(1)}, u32[]{:S(2)}, u32[]{:S(2)}) async-start(f32[64,4,128]{2,1,0:T(4,128)} %bitcast.31), calls=%async_computation.1 | async-start | bytes 262144 | tf_op jit(solution)/shard_map/all_to_all | solution.py:266
  158.3 8.1 %copy-start.4 = (s32[128]{0:T(128)S(1)}, s32[128]{0:T(128)}, u32[]{:S(2)}) copy-start(s32[128]{0:T(128)} %param.19) | copy-start | bytes 1540

commit v2 on v1

--- a/solution.py
+++ b/solution.py
@@ -164,16 +164,68 @@
     )(*args)
 
 
-def exchange(faces):
-    received = []
-    for face, (axis, step) in zip(faces, SIDES):
-        ends = lax.axis_size(axis) - 1
-        if step == 1:
-            pairs = [(i, i + 1) for i in range(ends)]
-        else:
-            pairs = [(i + 1, i) for i in range(ends)]
-        received.append(lax.ppermute(face, axis, pairs))
-    return received
+def halo_kernel(*refs):
+    sources, landings, (send_sem, recv_sem) = refs[:6], refs[6:12], refs[12:]
+    barrier = pltpu.get_barrier_semaphore()
+    routes = []
+    greeted = 0
+    for axis, step in SIDES:
+        count = lax.axis_size(axis)
+        place = lax.axis_index(axis)
+        above, below = place < count - 1, place > 0
+        sends, receives = (above, below) if step == 1 else (below, above)
+        routes.append((sends, receives, {axis: lax.rem(place + step + count, count)}))
+        greeted = greeted + jnp.where(sends, 1, 0)
+    for sends, _, target in routes:
+
+        @pl.when(sends)
+        def _greet():
+            pl.semaphore_signal(
+                barrier, inc=1, device_id=target, device_id_type=pl.DeviceIdType.MESH
+            )
+
+    pl.semaphore_wait(barrier, greeted)
+
+    def copy(k):
+        return pltpu.make_async_remote_copy(
+            src_ref=sources[k],
+            dst_ref=landings[k],
+            send_sem=send_sem.at[k],
+            recv_sem=recv_sem.at[k],
+            device_id=routes[k][2],
+            device_id_type=pl.DeviceIdType.MESH,
+        )
+
+    for k, (sends, receives, _) in enumerate(routes):
+
+        @pl.when(sends)
+        def _start():
+            copy(k).start()
+
+        @pl.when(jnp.logical_not(receives))
+        def _outside():
+            landings[k][...] = jnp.zeros_like(landings[k])
+
+    for k, (sends, receives, _) in enumerate(routes):
+
+        @pl.when(receives)
+        def _landed():
+            copy(k).wait_recv()
+
+        @pl.when(sends)
+        def _left():
+            copy(k).wait_send()
+
+
+def exchange(faces, index):
+    return pl.pallas_call(
+        halo_kernel,
+        out_shape=[jax.ShapeDtypeStruct(f.shape, f.dtype) for f in faces],
+        in_specs=[pl.BlockSpec(memory_space=VMEM)] * 6,
+        out_specs=[pl.BlockSpec(memory_space=VMEM)] * 6,
+        scratch_shapes=[pltpu.SemaphoreType.DMA((6,)), pltpu.SemaphoreType.DMA((6,))],
+        compiler_params=pltpu.CompilerParams(collective_id=index, has_side_effects=True),
+    )(*faces)
 
 
 def smooth(velocity, rhs, viscosity, faces, low, high):
@@ -182,7 +234,7 @@
     sigma_ratio = centre / half_width
     rho_now = 1.0 / sigma_ratio
     grid = (EX, EY, EZ)
-    visc_faces = exchange(faces)
+    visc_faces = exchange(faces, 0)
     field, update, field_faces = velocity, None, None
     for index in range(SWEEPS):
         first, last = index == 0, index == SWEEPS - 1
@@ -205,7 +257,7 @@
         if last:
             return results
         field, update = results[:2]
-        field_faces = exchange(results[2:])
+        field_faces = exchange(results[2:], index + 1)
 
 
 def one_hot_cells(cells):

time: 168 us -> 144 us (0.86)
  the two profiles are of different devices: /device:TPU:40 before, /device:TPU:1 now
where the time goes in v2:
time: 144 us; the launch traced here: 142 us
  Pallas kernels  42 us (29%)
  local copies, waits for them, and re-layouts  26.8 us (19%)
  waiting for transfers between devices  26.3 us (18%)
  starting transfers between devices  24 us (17%)
  matrix products  13.8 us (10%)
  other arithmetic  6.39 us (4%)
  between operations  2.57 us (2%)
    unnamed x94, local copies, waits for them, and re-layouts  24 us
    pallas_call x3, Pallas kernels, exchange(): pl.pallas_call(halo_kernel, out_shape=[jax.ShapeDtypeStruct(f.shape, f.dt...  23.4 us
    pallas_call x5, Pallas kernels, call(): pl.pallas_call(kernel, out_shape=[jax.ShapeDtypeStruct(s, jnp.float32) fo...  18.6 us
    all_to_all x1, starting transfers between devices, body(): lax.all_to_all(outgoing, ('gy', 'gz'), split_axis=0, concat_axis=0, tiled...  15.5 us
    all_to_all x1, waiting for transfers between devices, body(): lax.all_to_all(outgoing, ('gy', 'gz'), split_axis=0, concat_axis=0, tiled...  15.3 us
    all_to_all x1, waiting for transfers between devices, body(): lax.all_to_all(returning, ('gy', 'gz'), split_axis=0, concat_axis=0, tile...  11 us
    all_to_all x1, starting transfers between devices, body(): lax.all_to_all(returning, ('gy', 'gz'), split_axis=0, concat_axis=0, tile...  8.51 us
    dot_general x2, matrix products, interpolate(): jnp.einsum('gsk,gk->gs', one_hot_cells(cells), values, precision=lax.Prec...  7.99 us
  transfers between devices with their start and end apart: 2, of which 2 were waited for; matrix products, arithmetic and copies ran while one was open for 0% of the time, Pallas kernels for 0%

profile of v2, /device:TPU:1, one launch (start us, length us, event | category | flops | bytes accessed | tf_op | source)
XLA Modules:
  0.0 141.9 jit_solution(7775074357874467157)
XLA Ops:
  0.6 0.8 fusion.10
  1.6 0.9 select_reduce_fusion
  2.5 0.7 bitcast_add_fusion.flat_ref
  3.1 0.7 convert_element_type.26
  3.8 1.0 fusion.16
  5.0 6.0 %while.20 = (s32[]{:T(128)}, f32[2,64,3,128]{3,1,0,2:T(8,128)S(1)}, f32[2,3,64,128]{3,1,2,0:T(4,128)S(1)}, s32[2,64,128]{2,1,0:T(8,128)S(1)}, s32[]{:T(128)}) while((s32[]{:T(128)}, f32[2,64,3,128]{3,1,0,2:T(8,128)S(1)}, f32[2,3,64,128]{3,1,2,0:T(4,128)S(1)}, s32[2,64,128]{2,1,0:T(8,128)S(1)}, s32[]{:T(128)}) %tuple.42), condition=%wide.region_3.4_spmd, body=%wide.region_2.3_spmd.sunk | while | flops 38797312 | bytes 557137 | solution.py:296
  5.0 2.9 %fusion.24 = f32[1,64,3,128]{3,2,1,0:T(4,128)S(1)} fusion(s32[64,128]{1,0:T(8,128)S(1)} %dynamic-slice_bitcast_fusion.4, f32[2,3,64,128]{3,1,2,0:T(4,128)S(1)} %get-tuple-element.216, s32[]{:T(128)S(6)} %copy.31), kind=kOutput, calls=%fused_computation.5.clone.1 | convolution fusion | flops 38797312 | bytes 262148 | tf_op jit(solution)/shard_map/while/body/eval_jaxpr/gsk,cgs->gck/dot_general | solution.py:292
  8.0 2.9 %fusion.24 = f32[1,64,3,128]{3,2,1,0:T(4,128)S(1)} fusion(s32[64,128]{1,0:T(8,128)S(1)} %dynamic-slice_bitcast_fusion.4, f32[2,3,64,128]{3,1,2,0:T(4,128)S(1)} %get-tuple-element.216, s32[]{:T(128)S(6)} %copy.31), kind=kOutput, calls=%fused_computation.5.clone.1 | convolution fusion | flops 38797312 | bytes 262148 | tf_op jit(solution)/shard_map/while/body/eval_jaxpr/gsk,cgs->gck/dot_general | solution.py:292
  11.0 1.8 %shard_map.113 = f32[64,16,128]{2,1,0:T(8,128)} custom-call(s32[1,128]{1,0:T(1,128)S(1)} %bitcast_add_fusion.flat_ref, f32[128,128]{1,0:T(8,128)S(1)} %broadcast_in_dim.20.tile_ref, f32[3,128,128]{2,1,0:T(8,128)S(1)} %bitcast.86), custom_call_target="tpu_custom_call" | custom-call | tf_op jit(solution)/shard_map/pallas_call | solution.py:157
  12.8 15.5 %all-to-all-start = ((f32[64,16,128]{2,1,0:T(8,128)}), f32[64,16,128]{2,1,0:T(8,128)S(1)}, u32[]{:S(2)}, u32[]{:S(2)}) async-start(f32[64,16,128]{2,1,0:T(8,128)} %shard_map.113), calls=%async_computation | async-start | bytes 1048576 | tf_op jit(solution)/shard_map/all_to_all | solution.py:306
  30.1 15.3 %all-to-all-done.inc_ref = f32[64,16,128]{2,1,0:T(8,128)S(1)} async-done(((f32[64,16,128]{2,1,0:T(8,128)}), f32[64,16,128]{2,1,0:T(8,128)S(1)}, u32[]{:S(2)}, u32[]{:S(2)}) %all-to-all-start) | async-done | bytes 524320 | tf_op jit(solution)/shard_map/all_to_all | solution.py:306
  45.4 1.2 fusion.8
  46.9 7.1 %shard_map.114 = (f32[32,32,128]{2,1,0:T(8,128)S(1)}, f32[32,32,128]{2,1,0:T(8,128)S(1)}, f32[2,32,128]{2,1,0:T(8,128)S(1)}, f32[2,32,128]{2,1,0:T(8,128)S(1)}, ...) custom-call(s32[256]{0:T(256)S(1)} %convert_element_type.28.tile_ref, ...), custom_call_target="tpu_custom_call" | custom-call | tf_op jit(solution)/shard_map/pallas_call | solution.py:157
  55.2 0.6 copy-done.15
  55.8 0.6 copy-done.16
  57.0 0.6 copy-done.18
  57.6 9.2 %shard_map.115 = (f32[2,32,128]{2,1,0:T(8,128)}, f32[2,32,128]{2,1,0:T(8,128)}, f32[2,32,128]{2,1,0:T(8,128)}, f32[2,32,128]{2,1,0:T(8,128)}, f32[2,32,32]{2,1,0:T(8,128)}, /*index=5*/f32[2,32,32]{2,1,0:T(8,128)}) custom-call(f32[2,32,128]{2,1,0:T(8,128)} %copy-done.13, f32[2,32,128]{2,1,0:T(8,128)} %copy-done.14, f32[2,32,128]{2,1,0:T(8,128)} %copy-done.15, ...), custom_call_target="tpu_custom_call" | custom-call | tf_op jit(solution)/shard_map/pallas_call | solution.py:221
  66.8 0.7 copy-done.1
  67.6 0.8 copy-done.3
  68.3 0.8 copy-done.5
  69.1 0.8 copy-done.7
  69.8 0.8 copy-done.9
  70.6 0.8 copy-done.11
  71.4 2.3 %shard_map.116 = (f32[32,32,128]{2,1,0:T(8,128)S(1)}, f32[32,32,128]{2,1,0:T(8,128)S(1)}, f32[1,32,128]{2,1,0:T(8,128)S(1)}, f32[1,32,128]{2,1,0:T(8,128)S(1)}, ...) custom-call(f32[2]{0:T(128)S(1)} %pad_maximum_fusion.2.coef_ref, ...), custom_call_target="tpu_custom_call" | custom-call | tf_op jit(solution)/shard_map/pallas_call | solution.py:157
  77.3 6.7 %shard_map.117 = (f32[1,32,128]{2,1,0:T(8,128)}, f32[1,32,128]{2,1,0:T(8,128)}, f32[1,32,128]{2,1,0:T(8,128)}, f32[1,32,128]{2,1,0:T(8,128)}, f32[1,32,32]{2,1,0:T(8,128)}, /*index=5*/f32[1,32,32]{2,1,0:T(8,128)}) custom-call(f32[1,32,128]{2,1,0:T(8,128)} %copy-done.37, f32[1,32,128]{2,1,0:T(8,128)} %copy-done.38, f32[1,32,128]{2,1,0:T(8,128)} %copy-done.39, ...), custom_call_target="tpu_custom_call" | custom-call | tf_op jit(solution)/shard_map/pallas_call | solution.py:221
  84.0 0.7 copy-done.25
  84.7 0.7 copy-done.26
  85.5 0.7 copy-done.27
  86.2 0.7 copy-done.28
  86.9 0.7 copy-done.29
  87.6 0.7 copy-done.30
  88.3 2.3 %shard_map.118 = (f32[32,32,128]{2,1,0:T(8,128)S(1)}, f32[32,32,128]{2,1,0:T(8,128)S(1)}, f32[1,32,128]{2,1,0:T(8,128)S(1)}, f32[1,32,128]{2,1,0:T(8,128)S(1)}, ...) custom-call(f32[2]{0:T(128)S(1)} %pad_maximum_fusion.1.coef_ref, ...), custom_call_target="tpu_custom_call" | custom-call | tf_op jit(solution)/shard_map/pallas_call | solution.py:157
  94.2 7.5 %shard_map.119 = (f32[1,32,128]{2,1,0:T(8,128)}, f32[1,32,128]{2,1,0:T(8,128)}, f32[1,32,128]{2,1,0:T(8,128)}, f32[1,32,128]{2,1,0:T(8,128)}, f32[1,32,32]{2,1,0:T(8,128)}, /*index=5*/f32[1,32,32]{2,1,0:T(8,128)}) custom-call(f32[1,32,128]{2,1,0:T(8,128)} %copy-done.31, f32[1,32,128]{2,1,0:T(8,128)} %copy-done.32, f32[1,32,128]{2,1,0:T(8,128)} %copy-done.33, ...), custom_call_target="tpu_custom_call" | custom-call | tf_op jit(solution)/shard_map/pallas_call | solution.py:221
  101.8 0.7 copy-done.19
  102.5 0.7 copy-done.20
  103.2 0.7 copy-done.21
  103.9 0.7 copy-done.22
  104.7 0.7 copy-done.23
  105.4 0.7 copy-done.24
  106.1 5.2 %shard_map.120 = (f32[32,32,128]{2,1,0:T(8,128)}, f32[1024,128]{1,0:T(8,128)S(1)}) custom-call(f32[2]{0:T(128)S(1)} %pad_maximum_fusion.coef_ref, f32[32,32,128]{2,1,0:T(8,128)S(1)} %get-tuple-element.119.field_ref, f32[32,32,128]{2,1,0:T(8,128)S(1)} %get-tuple-element.91.rhs_ref, f32[32,32,128]{2,1,0:T(8,128)S(1)} %get-tuple-element.92.visc_ref, ...), custom_call_target="tpu_custom_call" | custom-call | tf_op jit(solution)/shard_map/pallas_call | solution.py:157
  111.3 1.3 gather_fusion
  112.6 8.5 %all-to-all-start.1 = ((f32[64,4,128]{2,1,0:T(4,128)}), f32[64,4,128]{2,1,0:T(4,128)S(1)}, u32[]{:S(2)}, u32[]{:S(2)}) async-start(f32[64,4,128]{2,1,0:T(4,128)} %bitcast.31), calls=%async_computation.1 | async-start | bytes 262144 | tf_op jit(solution)/shard_map/all_to_all | solution.py:318
  121.2 11.0 %all-to-all-done.1 = f32[64,4,128]{2,1,0:T(4,128)S(1)} async-done(((f32[64,4,128]{2,1,0:T(4,128)}), f32[64,4,128]{2,1,0:T(4,128)S(1)}, u32[]{:S(2)}, u32[]{:S(2)}) %all-to-all-start.1) | async-done | bytes 131104 | tf_op jit(solution)/shard_map/all_to_all | solution.py:318
  132.1 1.0 gather_fusion.1
  133.1 8.1 %while.21 = (s32[]{:T(128)}, f32[2,64,128]{2,1,0:T(8,128)S(1)}, s32[2,64,128]{2,1,0:T(8,128)S(1)}, f32[2,64,128]{2,1,0:T(8,128)S(1)}, s32[]{:T(128)}) while((s32[]{:T(128)}, f32[2,64,128]{2,1,0:T(8,128)S(1)}, s32[2,64,128]{2,1,0:T(8,128)S(1)}, f32[2,64,128]{2,1,0:T(8,128)S(1)}, s32[]{:T(128)}) %tuple.44), condition=%wide.region_5.6_spmd, body=%wide.region_4.5_spmd.sunk | while | flops 13631490 | bytes 294993 | solution.py:327
  133.2 4.0 %fusion.26 = f32[64,1,128]{2,1,0:T(1,128)S(1)} fusion(f32[64,128,1]{1,2,0:T(1,128)S(1)} %bitcast.81, s32[64,128]{1,0:T(8,128)S(1)} %dynamic-slice_bitcast_fusion.5), kind=kOutput, calls=%fused_computation.12.clone.1 | convolution fusion | flops 13631488 | bytes 98304 | tf_op jit(solution)/shard_map/while/body/eval_jaxpr/gsk,gk->gs/dot_general | solution.py:323
  137.2 4.0 %fusion.26 = f32[64,1,128]{2,1,0:T(1,128)S(1)} fusion(f32[64,128,1]{1,2,0:T(1,128)S(1)} %bitcast.81, s32[64,128]{1,0:T(8,128)S(1)} %dynamic-slice_bitcast_fusion.5), kind=kOutput, calls=%fused_computation.12.clone.1 | convolution fusion | flops 13631488 | bytes 98304 | tf_op jit(solution)/shard_map/while/body/eval_jaxpr/gsk,gk->gs/dot_general | solution.py:323
  141.2 0.7 bitcast_select_fusion
  (97 shorter events, 10.1 us)
Async XLA Ops:
  0.6 4.1 %copy-start.44 = (f32[128,128]{1,0:T(8,128)S(1)}, f32[128,128]{1,0:T(8,128)}, u32[]{:S(2)}) copy-start(f32[128,128]{1,0:T(8,128)} %param.16) | copy-start | bytes 196612
  1.6 3.4 %copy-start.43 = (s32[128,128]{1,0:T(8,128)S(1)}, s32[128,128]{1,0:T(8,128)}, u32[]{:S(2)}) copy-start(s32[128,128]{1,0:T(8,128)} %param.18) | copy-start | bytes 196612
  12.8 34.0 %copy-start = (f32[32,32,128]{2,1,0:T(8,128)S(1)}, f32[32,32,128]{2,1,0:T(8,128)}, u32[]{:S(2)}) copy-start(f32[32,32,128]{2,1,0:T(8,128)} %field_ref.1) | copy-start | bytes 1572868
  12.8 32.6 %all-to-all-start = ((f32[64,16,128]{2,1,0:T(8,128)}), f32[64,16,128]{2,1,0:T(8,128)S(1)}, u32[]{:S(2)}, u32[]{:S(2)}) async-start(f32[64,16,128]{2,1,0:T(8,128)} %shard_map.113), calls=%async_computation | async-start | bytes 1048576 | tf_op jit(solution)/shard_map/all_to_all | solution.py:306
  53.9 0.6 copy-start.13
  54.5 0.6 copy-start.14
  55.2 0.6 copy-start.15
  55.8 0.6 copy-start.16
  56.4 0.6 copy-start.17
  57.0 0.6 copy-start.18
  66.8 0.8 copy-start.1
  67.5 0.8 copy-start.3
  68.3 0.8 copy-start.5
  69.1 0.8 copy-start.7
  69.8 0.8 copy-start.9
  70.6 0.8 copy-start.11
  71.3 12.6 %copy-start.2 = (f32[2,32,128]{2,1,0:T(8,128)S(1)}, f32[2,32,128]{2,1,0:T(8,128)}, u32[]{:S(2)}) copy-start(f32[2,32,128]{2,1,0:T(8,128)} %get-tuple-element.99.rest_0_) | copy-start | bytes 98308
  71.3 12.6 %copy-start.4 = (f32[2,32,128]{2,1,0:T(8,128)S(1)}, f32[2,32,128]{2,1,0:T(8,128)}, u32[]{:S(2)}) copy-start(f32[2,32,128]{2,1,0:T(8,128)} %get-tuple-element.100.rest_1_) | copy-start | bytes 98308
  71.3 12.6 %copy-start.6 = (f32[2,32,128]{2,1,0:T(8,128)S(1)}, f32[2,32,128]{2,1,0:T(8,128)}, u32[]{:S(2)}) copy-start(f32[2,32,128]{2,1,0:T(8,128)} %get-tuple-element.101.rest_2_) | copy-start | bytes 98308
  71.3 12.6 %copy-start.8 = (f32[2,32,128]{2,1,0:T(8,128)S(1)}, f32[2,32,128]{2,1,0:T(8,128)}, u32[]{:S(2)}) copy-start(f32[2,32,128]{2,1,0:T(8,128)} %get-tuple-element.102.rest_3_) | copy-start | bytes 98308
  71.4 12.7 %copy-start.10 = (f32[2,32,32]{2,1,0:T(8,128)S(1)}, f32[2,32,32]{2,1,0:T(8,128)}, u32[]{:S(2)}) copy-start(f32[2,32,32]{2,1,0:T(8,128)} %get-tuple-element.103.rest_4_) | copy-start | bytes 24580
  71.4 12.7 %copy-start.12 = (f32[2,32,32]{2,1,0:T(8,128)S(1)}, f32[2,32,32]{2,1,0:T(8,128)}, u32[]{:S(2)}) copy-start(f32[2,32,32]{2,1,0:T(8,128)} %get-tuple-element.104.rest_5_) | copy-start | bytes 24580
  73.7 0.6 copy-start.37
  74.3 0.6 copy-start.38
  74.9 0.6 copy-start.39
  75.5 0.6 copy-start.40
  76.1 0.6 copy-start.41
  76.7 0.6 copy-start.42
  84.0 0.7 copy-start.25
  84.7 0.7 copy-start.26
  85.5 0.7 copy-start.27
  86.2 0.7 copy-start.28
  86.9 0.7 copy-start.29
  87.6 0.7 copy-start.30
  90.6 0.6 copy-start.31
  91.2 0.6 copy-start.32
  92.4 0.6 copy-start.34
  93.0 0.6 copy-start.35
  93.6 0.6 copy-start.36
  101.8 0.7 copy-start.19
  102.5 0.7 copy-start.20
  103.2 0.7 copy-start.21
  103.9 0.7 copy-start.22
  104.7 0.7 copy-start.23
  105.4 0.7 copy-start.24
  111.3 9.9 %copy-start.45 = (s32[128,1]{0,1:T(1,128)S(1)}, s32[128,1]{0,1:T(1,128)}, u32[]{:S(2)}) copy-start(s32[128,1]{0,1:T(1,128)} %param.20) | copy-start | bytes 1540
  112.6 19.5 %all-to-all-start.1 = ((f32[64,4,128]{2,1,0:T(4,128)}), f32[64,4,128]{2,1,0:T(4,128)S(1)}, u32[]{:S(2)}, u32[]{:S(2)}) async-start(f32[64,4,128]{2,1,0:T(4,128)} %bitcast.31), calls=%async_computation.1 | async-start | bytes 262144 | tf_op jit(solution)/shard_map/all_to_all | solution.py:318
  133.1 8.1 %copy-start.46 = (s32[128]{0:T(128)S(1)}, s32[128]{0:T(128)}, u32[]{:S(2)}) copy-start(s32[128]{0:T(128)} %param.19) | copy-start | bytes 1540
  (1 other events, 0.6 us)

commit v3 on v2

--- a/solution.py
+++ b/solution.py
@@ -151,6 +151,16 @@
         return carry
 
     lax.fori_loop(0, 8, gather, 0)
+
+
+def pick_kernel(values_ref, cell_ref, count_ref, out_ref):
+    for start in range(0, out_ref.shape[0], 8):
+        rows = slice(start, start + 8)
+        picked = jnp.take_along_axis(
+            values_ref[rows, :], cell_ref[rows, :], axis=1, mode="promise_in_bounds"
+        )
+        slot = lax.broadcasted_iota(jnp.int32, picked.shape, 1)
+        out_ref[rows, :] = jnp.where(slot < count_ref[rows, :], picked, 0.0)
 
 
 def call(kernel, outs, specs, args, scratch=()):
@@ -316,16 +326,13 @@
     smoothed, tile_view = smooth(velocity, rhs, viscosity, results[2:], eig_low[0], eig_high[0])
     returning = tile_view[tile_in].reshape(owners, capacity, TILE_CELLS)
     arrived = lax.all_to_all(returning, ("gy", "gz"), split_axis=0, concat_axis=0, tiled=True)
-    block_values = arrived[owner, slot_of].reshape(groups, group, TILE_CELLS)
-
-    def interpolate(pair):
-        cells, values = pair
-        return jnp.einsum(
-            "gsk,gk->gs", one_hot_cells(cells), values, precision=lax.Precision.HIGHEST
-        )
-
-    picked = lax.map(interpolate, (cells_grouped, block_values)).reshape(blocks, slots)
-    marker_velocity = jnp.where(live, picked, 0.0)
+    counts = jnp.broadcast_to(block_count[:, None], (blocks, slots))
+    (marker_velocity,) = call(
+        pick_kernel,
+        [(blocks, slots)],
+        [VMEM] * 3,
+        [arrived[owner, slot_of], marker_cell, counts],
+    )
     return (smoothed, marker_velocity)
 
 

time: 144 us -> 135 us (0.938)
  the two profiles are of different devices: /device:TPU:1 before, /device:TPU:16 now
where the time goes in v3:
time: 135 us; the launch traced here: 133 us
  Pallas kernels  41.1 us (30%)
  waiting for transfers between devices  28.3 us (21%)
  local copies, waits for them, and re-layouts  26.7 us (20%)
  starting transfers between devices  22.8 us (17%)
  matrix products  5.84 us (4%)
  other arithmetic  5.67 us (4%)
  between operations  2.56 us (2%)
    unnamed x94, local copies, waits for them, and re-layouts  24 us
    pallas_call x3, Pallas kernels, exchange(): pl.pallas_call(halo_kernel, out_shape=[jax.ShapeDtypeStruct(f.shape, f.dt...  21.9 us
    pallas_call x6, Pallas kernels, call(): pl.pallas_call(kernel, out_shape=[jax.ShapeDtypeStruct(s, jnp.float32) fo...  19.1 us
    all_to_all x1, waiting for transfers between devices, body(): lax.all_to_all(outgoing, ('gy', 'gz'), split_axis=0, concat_axis=0, tiled...  16.8 us
    all_to_all x1, starting transfers between devices, body(): lax.all_to_all(outgoing, ('gy', 'gz'), split_axis=0, concat_axis=0, tiled...  14.9 us
    all_to_all x1, waiting for transfers between devices, body(): lax.all_to_all(returning, ('gy', 'gz'), split_axis=0, concat_axis=0, tile...  11.5 us
    all_to_all x1, starting transfers between devices, body(): lax.all_to_all(returning, ('gy', 'gz'), split_axis=0, concat_axis=0, tile...  7.83 us
    dot_general x2, matrix products, project(): jnp.einsum('gsk,cgs->gck', one_hot_cells(cells), values, precision=lax.Pr...  5.84 us
  transfers between devices with their start and end apart: 2, of which 2 were waited for; matrix products, arithmetic and copies ran while one was open for 0% of the time, Pallas kernels for 0%

profile of v3, /device:TPU:16, one launch (start us, length us, event | category | flops | bytes accessed | tf_op | source)
XLA Modules:
  0.0 133.0 jit_solution(7186751566128811449)
XLA Ops:
  0.6 0.8 fusion.7
  1.6 0.9 select_reduce_fusion
  2.5 0.7 bitcast_add_fusion.flat_ref
  3.1 0.7 convert_element_type.25
  3.8 1.0 fusion.14
  5.0 6.0 %while.10 = (s32[]{:T(128)}, f32[2,64,3,128]{3,1,0,2:T(8,128)S(1)}, f32[2,3,64,128]{3,1,2,0:T(4,128)S(1)}, s32[2,64,128]{2,1,0:T(8,128)S(1)}, s32[]{:T(128)}) while((s32[]{:T(128)}, f32[2,64,3,128]{3,1,0,2:T(8,128)S(1)}, f32[2,3,64,128]{3,1,2,0:T(4,128)S(1)}, s32[2,64,128]{2,1,0:T(8,128)S(1)}, s32[]{:T(128)}) %tuple.26), condition=%wide.region_3.4_spmd, body=%wide.region_2.3_spmd.sunk | while | flops 38797312 | bytes 557137 | solution.py:306
  5.0 2.9 %fusion.19 = f32[1,64,3,128]{3,2,1,0:T(4,128)S(1)} fusion(s32[64,128]{1,0:T(8,128)S(1)} %dynamic-slice_bitcast_fusion.2, f32[2,3,64,128]{3,1,2,0:T(4,128)S(1)} %get-tuple-element.160, s32[]{:T(128)S(6)} %copy.28), kind=kOutput, calls=%fused_computation.5.clone.1 | convolution fusion | flops 38797312 | bytes 262148 | tf_op jit(solution)/shard_map/while/body/eval_jaxpr/gsk,cgs->gck/dot_general | solution.py:302
  8.0 2.9 %fusion.19 = f32[1,64,3,128]{3,2,1,0:T(4,128)S(1)} fusion(s32[64,128]{1,0:T(8,128)S(1)} %dynamic-slice_bitcast_fusion.2, f32[2,3,64,128]{3,1,2,0:T(4,128)S(1)} %get-tuple-element.160, s32[]{:T(128)S(6)} %copy.28), kind=kOutput, calls=%fused_computation.5.clone.1 | convolution fusion | flops 38797312 | bytes 262148 | tf_op jit(solution)/shard_map/while/body/eval_jaxpr/gsk,cgs->gck/dot_general | solution.py:302
  11.0 1.8 %shard_map.113 = f32[64,16,128]{2,1,0:T(8,128)} custom-call(s32[1,128]{1,0:T(1,128)S(1)} %bitcast_add_fusion.flat_ref, f32[128,128]{1,0:T(8,128)S(1)} %broadcast_in_dim.14.tile_ref, f32[3,128,128]{2,1,0:T(8,128)S(1)} %bitcast.61), custom_call_target="tpu_custom_call" | custom-call | tf_op jit(solution)/shard_map/pallas_call | solution.py:167
  12.8 14.9 %all-to-all-start = ((f32[64,16,128]{2,1,0:T(8,128)}), f32[64,16,128]{2,1,0:T(8,128)S(1)}, u32[]{:S(2)}, u32[]{:S(2)}) async-start(f32[64,16,128]{2,1,0:T(8,128)} %shard_map.113), calls=%async_computation | async-start | bytes 1048576 | tf_op jit(solution)/shard_map/all_to_all | solution.py:316
  29.6 16.8 %all-to-all-done.inc_ref = f32[64,16,128]{2,1,0:T(8,128)S(1)} async-done(((f32[64,16,128]{2,1,0:T(8,128)}), f32[64,16,128]{2,1,0:T(8,128)S(1)}, u32[]{:S(2)}, u32[]{:S(2)}) %all-to-all-start) | async-done | bytes 524320 | tf_op jit(solution)/shard_map/all_to_all | solution.py:316
  46.4 1.2 fusion.6
  47.8 6.8 %shard_map.114 = (f32[32,32,128]{2,1,0:T(8,128)S(1)}, f32[32,32,128]{2,1,0:T(8,128)S(1)}, f32[2,32,128]{2,1,0:T(8,128)S(1)}, f32[2,32,128]{2,1,0:T(8,128)S(1)}, ...) custom-call(s32[256]{0:T(256)S(1)} %convert_element_type.27.tile_ref, ...), custom_call_target="tpu_custom_call" | custom-call | tf_op jit(solution)/shard_map/pallas_call | solution.py:167
  54.6 0.6 copy-done.13
  55.3 0.6 copy-done.14
  56.5 0.6 copy-done.16
  57.1 0.6 copy-done.17
  57.7 0.6 copy-done.18
  58.3 6.6 %shard_map.115 = (f32[2,32,128]{2,1,0:T(8,128)}, f32[2,32,128]{2,1,0:T(8,128)}, f32[2,32,128]{2,1,0:T(8,128)}, f32[2,32,128]{2,1,0:T(8,128)}, f32[2,32,32]{2,1,0:T(8,128)}, /*index=5*/f32[2,32,32]{2,1,0:T(8,128)}) custom-call(f32[2,32,128]{2,1,0:T(8,128)} %copy-done.13, f32[2,32,128]{2,1,0:T(8,128)} %copy-done.14, f32[2,32,128]{2,1,0:T(8,128)} %copy-done.15, ...), custom_call_target="tpu_custom_call" | custom-call | tf_op jit(solution)/shard_map/pallas_call | solution.py:231
  64.9 0.7 copy-done.1
  65.6 0.8 copy-done.3
  66.4 0.8 copy-done.5
  67.1 0.8 copy-done.7
  67.9 0.8 copy-done.9
  68.7 0.8 copy-done.11
  69.4 2.3 %shard_map.116 = (f32[32,32,128]{2,1,0:T(8,128)S(1)}, f32[32,32,128]{2,1,0:T(8,128)S(1)}, f32[1,32,128]{2,1,0:T(8,128)S(1)}, f32[1,32,128]{2,1,0:T(8,128)S(1)}, ...) custom-call(f32[2]{0:T(128)S(1)} %pad_maximum_fusion.2.coef_ref, ...), custom_call_target="tpu_custom_call" | custom-call | tf_op jit(solution)/shard_map/pallas_call | solution.py:167
  72.4 0.6 copy-done.38
  75.4 7.2 %shard_map.117 = (f32[1,32,128]{2,1,0:T(8,128)}, f32[1,32,128]{2,1,0:T(8,128)}, f32[1,32,128]{2,1,0:T(8,128)}, f32[1,32,128]{2,1,0:T(8,128)}, f32[1,32,32]{2,1,0:T(8,128)}, /*index=5*/f32[1,32,32]{2,1,0:T(8,128)}) custom-call(f32[1,32,128]{2,1,0:T(8,128)} %copy-done.37, f32[1,32,128]{2,1,0:T(8,128)} %copy-done.38, f32[1,32,128]{2,1,0:T(8,128)} %copy-done.39, ...), custom_call_target="tpu_custom_call" | custom-call | tf_op jit(solution)/shard_map/pallas_call | solution.py:231
  82.6 0.7 copy-done.25
  83.3 0.7 copy-done.26
  84.0 0.7 copy-done.27
  84.7 0.7 copy-done.28
  85.5 0.7 copy-done.29
  86.2 0.7 copy-done.30
  86.9 2.3 %shard_map.118 = (f32[32,32,128]{2,1,0:T(8,128)S(1)}, f32[32,32,128]{2,1,0:T(8,128)S(1)}, f32[1,32,128]{2,1,0:T(8,128)S(1)}, f32[1,32,128]{2,1,0:T(8,128)S(1)}, ...) custom-call(f32[2]{0:T(128)S(1)} %pad_maximum_fusion.1.coef_ref, ...), custom_call_target="tpu_custom_call" | custom-call | tf_op jit(solution)/shard_map/pallas_call | solution.py:167
  92.8 8.2 %shard_map.119 = (f32[1,32,128]{2,1,0:T(8,128)}, f32[1,32,128]{2,1,0:T(8,128)}, f32[1,32,128]{2,1,0:T(8,128)}, f32[1,32,128]{2,1,0:T(8,128)}, f32[1,32,32]{2,1,0:T(8,128)}, /*index=5*/f32[1,32,32]{2,1,0:T(8,128)}) custom-call(f32[1,32,128]{2,1,0:T(8,128)} %copy-done.31, f32[1,32,128]{2,1,0:T(8,128)} %copy-done.32, f32[1,32,128]{2,1,0:T(8,128)} %copy-done.33, ...), custom_call_target="tpu_custom_call" | custom-call | tf_op jit(solution)/shard_map/pallas_call | solution.py:231
  101.0 0.7 copy-done.19
  101.8 0.7 copy-done.20
  102.5 0.7 copy-done.21
  103.2 0.7 copy-done.22
  103.9 0.7 copy-done.23
  104.6 0.7 copy-done.24
  105.3 5.2 %shard_map.120 = (f32[32,32,128]{2,1,0:T(8,128)}, f32[1024,128]{1,0:T(8,128)S(1)}) custom-call(f32[2]{0:T(128)S(1)} %pad_maximum_fusion.coef_ref, f32[32,32,128]{2,1,0:T(8,128)S(1)} %get-tuple-element.97.field_ref, f32[32,32,128]{2,1,0:T(8,128)S(1)} %get-tuple-element.69.rhs_ref, f32[32,32,128]{2,1,0:T(8,128)S(1)} %get-tuple-element.70.visc_ref, ...), custom_call_target="tpu_custom_call" | custom-call | tf_op jit(solution)/shard_map/pallas_call | solution.py:167
  110.5 1.3 %gather_fusion = f32[256,128]{1,0:T(8,128)} fusion(f32[1024,128]{1,0:T(8,128)S(1)} %get-tuple-element.112, s32[1024]{0:T(1024)S(1)} %pad_clamp_fusion), kind=kCustom, calls=%fused_computation | custom fusion | bytes 263168 | tf_op jit(solution)/shard_map/gather | solution.py:327
  111.8 7.8 %all-to-all-start.1 = ((f32[64,4,128]{2,1,0:T(4,128)}), f32[64,4,128]{2,1,0:T(4,128)S(1)}, u32[]{:S(2)}, u32[]{:S(2)}) async-start(f32[64,4,128]{2,1,0:T(4,128)} %bitcast.24), calls=%async_computation.1 | async-start | bytes 262144 | tf_op jit(solution)/shard_map/all_to_all | solution.py:328
  119.7 11.5 %all-to-all-done.1 = f32[64,4,128]{2,1,0:T(4,128)S(1)} async-done(((f32[64,4,128]{2,1,0:T(4,128)}), f32[64,4,128]{2,1,0:T(4,128)S(1)}, u32[]{:S(2)}, u32[]{:S(2)}) %all-to-all-start.1) | async-done | bytes 131104 | tf_op jit(solution)/shard_map/all_to_all | solution.py:328
  131.2 1.0 gather_fusion.1
  132.2 0.8 shard_map.121
  (88 shorter events, 8.3 us)
Async XLA Ops:
  0.6 4.1 %copy-start.44 = (f32[128,128]{1,0:T(8,128)S(1)}, f32[128,128]{1,0:T(8,128)}, u32[]{:S(2)}) copy-start(f32[128,128]{1,0:T(8,128)} %param.14) | copy-start | bytes 196612
  1.6 3.4 %copy-start.43 = (s32[128,128]{1,0:T(8,128)S(1)}, s32[128,128]{1,0:T(8,128)}, u32[]{:S(2)}) copy-start(s32[128,128]{1,0:T(8,128)} %cell_ref.1) | copy-start | bytes 196612
  12.8 35.0 %copy-start = (f32[32,32,128]{2,1,0:T(8,128)S(1)}, f32[32,32,128]{2,1,0:T(8,128)}, u32[]{:S(2)}) copy-start(f32[32,32,128]{2,1,0:T(8,128)} %field_ref.1) | copy-start | bytes 1572868
  12.8 33.6 %all-to-all-start = ((f32[64,16,128]{2,1,0:T(8,128)}), f32[64,16,128]{2,1,0:T(8,128)S(1)}, u32[]{:S(2)}, u32[]{:S(2)}) async-start(f32[64,16,128]{2,1,0:T(8,128)} %shard_map.113), calls=%async_computation | async-start | bytes 1048576 | tf_op jit(solution)/shard_map/all_to_all | solution.py:316
  54.6 0.6 copy-start.13
  55.3 0.6 copy-start.14
  55.9 0.6 copy-start.15
  56.5 0.6 copy-start.16
  57.1 0.6 copy-start.17
  57.7 0.6 copy-start.18
  64.9 0.8 copy-start.1
  65.6 0.8 copy-start.3
  66.4 0.8 copy-start.5
  67.1 0.8 copy-start.7
  67.9 0.8 copy-start.9
  68.7 0.8 copy-start.11
  69.4 13.1 %copy-start.2 = (f32[2,32,128]{2,1,0:T(8,128)S(1)}, f32[2,32,128]{2,1,0:T(8,128)}, u32[]{:S(2)}) copy-start(f32[2,32,128]{2,1,0:T(8,128)} %get-tuple-element.77.rest_0_) | copy-start | bytes 98308
  69.4 13.1 %copy-start.4 = (f32[2,32,128]{2,1,0:T(8,128)S(1)}, f32[2,32,128]{2,1,0:T(8,128)}, u32[]{:S(2)}) copy-start(f32[2,32,128]{2,1,0:T(8,128)} %get-tuple-element.78.rest_1_) | copy-start | bytes 98308
  69.4 13.1 %copy-start.6 = (f32[2,32,128]{2,1,0:T(8,128)S(1)}, f32[2,32,128]{2,1,0:T(8,128)}, u32[]{:S(2)}) copy-start(f32[2,32,128]{2,1,0:T(8,128)} %get-tuple-element.79.rest_2_) | copy-start | bytes 98308
  69.4 13.1 %copy-start.8 = (f32[2,32,128]{2,1,0:T(8,128)S(1)}, f32[2,32,128]{2,1,0:T(8,128)}, u32[]{:S(2)}) copy-start(f32[2,32,128]{2,1,0:T(8,128)} %get-tuple-element.80.rest_3_) | copy-start | bytes 98308
  69.4 13.1 %copy-start.10 = (f32[2,32,32]{2,1,0:T(8,128)S(1)}, f32[2,32,32]{2,1,0:T(8,128)}, u32[]{:S(2)}) copy-start(f32[2,32,32]{2,1,0:T(8,128)} %get-tuple-element.81.rest_4_) | copy-start | bytes 24580
  69.4 13.1 %copy-start.12 = (f32[2,32,32]{2,1,0:T(8,128)S(1)}, f32[2,32,32]{2,1,0:T(8,128)}, u32[]{:S(2)}) copy-start(f32[2,32,32]{2,1,0:T(8,128)} %get-tuple-element.82.rest_5_) | copy-start | bytes 24580
  71.7 0.6 copy-start.37
  72.4 0.6 copy-start.38
  73.0 0.6 copy-start.39
  73.6 0.6 copy-start.40
  74.2 0.6 copy-start.41
  74.8 0.6 copy-start.42
  82.6 0.7 copy-start.25
  83.3 0.7 copy-start.26
  84.0 0.7 copy-start.27
  84.7 0.7 copy-start.28
  85.5 0.7 copy-start.29
  86.2 0.7 copy-start.30
  89.2 0.6 copy-start.31
  89.8 0.6 copy-start.32
  90.4 0.6 copy-start.33
  91.6 0.6 copy-start.35
  92.2 0.6 copy-start.36
  101.0 0.7 copy-start.19
  101.8 0.7 copy-start.20
  102.5 0.7 copy-start.21
  103.2 0.7 copy-start.22
  103.9 0.7 copy-start.23
  104.6 0.7 copy-start.24
  110.5 9.2 %copy-start.45 = (s32[128,1]{0,1:T(1,128)S(1)}, s32[128,1]{0,1:T(1,128)}, u32[]{:S(2)}) copy-start(s32[128,1]{0,1:T(1,128)} %param.18) | copy-start | bytes 1540
  111.8 20.3 %copy-start.46 = (s32[128]{0:T(128)S(1)}, s32[128]{0:T(128)}, u32[]{:S(2)}) copy-start(s32[128]{0:T(128)} %param.17) | copy-start | bytes 1540
  111.8 19.3 %all-to-all-start.1 = ((f32[64,4,128]{2,1,0:T(4,128)}), f32[64,4,128]{2,1,0:T(4,128)S(1)}, u32[]{:S(2)}, u32[]{:S(2)}) async-start(f32[64,4,128]{2,1,0:T(4,128)} %bitcast.24), calls=%async_computation.1 | async-start | bytes 262144 | tf_op jit(solution)/shard_map/all_to_all | solution.py:328
  (1 other events, 0.6 us)
